TPU v7x, 32 devices: a whole 2x2x4 slice. The times are simulated.
32 devices in a mesh: row: 4 (over z), col: 8 (over y, x, core).
Axes of the slice: x: 2, y: 2, z: 4, core: 2. Of those that a mesh axis runs over, the one named last changes fastest.
Arguments:
- pair: bfloat16 [256, 256, 128], P('row', 'col'), may hold values from -6 to 6
- residue_mask: int32 [256], replicated, may hold values 0 or 1
- norm_gain: float32 [2, 2, 128], replicated, may hold values from 0.25 to 1.75
- norm_bias: float32 [2, 2, 128], replicated, may hold values from -3 to 3
- w_in_q: bfloat16 [2, 128, 640], replicated, may hold values from -0.5 to 0.5
- exp_in: int32 [2, 4, 20], replicated, may hold values from -2 to 1
- w_out_q: bfloat16 [2, 128, 128], replicated, may hold values from -0.5 to 0.5
- exp_out: int32 [2, 4, 4], replicated, may hold values from -2 to 1
Outputs:
- pair_out: bfloat16 [256, 256, 128], P('row', 'col')
All inputs are finite; a program needn't handle non-finite values.
Results may differ from a plain program's by a relative error of at most 0.0056.
Values may be sent and summed in bfloat16 or wider, within the bound.
No kernel may reach another device: no remote copies, remote signals or barrier semaphores. Data moves between devices by JAX's collectives and lax.ppermute only.
A program may use at most 128 MiB of HBM per device.

v0:
```python
import jax
import jax.numpy as jnp
from jax import lax
from jax.sharding import PartitionSpec as P

BLK = 32


def spread(x, axis, root):
    mine = lax.axis_index(axis) == root
    return lax.psum(jnp.where(mine, x, jnp.zeros_like(x)), axis)


def layer_norm(values, scale_vec, shift_vec):
    average = jnp.mean(values, axis=-1, keepdims=True)
    centred = values - average
    variance = jnp.mean(centred * centred, axis=-1, keepdims=True)
    return centred * lax.rsqrt(variance + 1e-05) * scale_vec + shift_vec


def dequantize(quantized, exponents, block_size):
    scales = jnp.exp2(exponents.astype(jnp.float32))
    scales = jnp.repeat(jnp.repeat(scales, block_size, axis=0), block_size, axis=1)
    return (quantized.astype(jnp.float32) * scales).astype(jnp.bfloat16)


def project(pair_in, row_mask, col_mask, layer, norm_gain, norm_bias, w_in_q, exp_in):
    rows_n, cols_n, width = pair_in.shape
    normed = layer_norm(
        pair_in.astype(jnp.float32), norm_gain[layer, 0], norm_bias[layer, 0]
    ).astype(jnp.bfloat16)
    weights_in = dequantize(w_in_q[layer], exp_in[layer], BLK)
    projected = jnp.dot(
        normed.reshape(rows_n * cols_n, width), weights_in, preferred_element_type=jnp.float32
    )
    projected = projected.reshape(rows_n, cols_n, 5 * width)
    pair_mask = (row_mask[:, None] * col_mask[None, :])[:, :, None]
    left = (
        jax.nn.sigmoid(projected[:, :, 0:width]) * projected[:, :, width : 2 * width] * pair_mask
    ).astype(jnp.bfloat16)
    right = (
        jax.nn.sigmoid(projected[:, :, 2 * width : 3 * width])
        * projected[:, :, 3 * width : 4 * width]
        * pair_mask
    ).astype(jnp.bfloat16)
    gate = jax.nn.sigmoid(projected[:, :, 4 * width :])
    return (left, right, gate)


def finish(pair_in, summed, gate, layer, norm_gain, norm_bias, w_out_q, exp_out):
    rows_n, cols_n, width = pair_in.shape
    normed = layer_norm(summed, norm_gain[layer, 1], norm_bias[layer, 1]).astype(jnp.bfloat16)
    weights_out = dequantize(w_out_q[layer], exp_out[layer], BLK)
    update = jnp.dot(
        normed.reshape(rows_n * cols_n, width), weights_out, preferred_element_type=jnp.float32
    )
    update = update.reshape(rows_n, cols_n, width)
    return (pair_in.astype(jnp.float32) + gate * update).astype(jnp.bfloat16)


def shards(pair, residue_mask, norm_gain, norm_bias, w_in_q, exp_in, w_out_q, exp_out):
    rows_n, cols_n, width = pair.shape
    row_count = lax.axis_size("row")
    col_count = lax.axis_size("col")
    col_ratio = col_count // row_count
    row_place = lax.axis_index("row")
    col_place = lax.axis_index("col")
    mask_all = residue_mask.astype(jnp.float32)
    row_mask = lax.dynamic_slice_in_dim(mask_all, row_place * rows_n, rows_n)
    col_mask = lax.dynamic_slice_in_dim(mask_all, col_place * cols_n, cols_n)
    left, right, gate = project(pair, row_mask, col_mask, 0, norm_gain, norm_bias, w_in_q, exp_in)
    right_panel = lax.all_gather(right, "col", axis=1, tiled=True)
    chosen = lax.dynamic_slice_in_dim(right_panel, col_place % col_ratio * cols_n, cols_n, 0)
    right_rows = spread(chosen, "row", col_place // col_ratio)
    selected = right_rows
    summed = jnp.einsum(
        "ikc,jkc->ijc",
        lax.all_gather(left, "col", axis=1, tiled=True),
        selected,
        preferred_element_type=jnp.float32,
    )
    pair_mid = finish(pair, summed, gate, 0, norm_gain, norm_bias, w_out_q, exp_out)
    left, right, gate = project(
        pair_mid, row_mask, col_mask, 1, norm_gain, norm_bias, w_in_q, exp_in
    )
    column_panel = lax.all_gather(left, "row", axis=0, tiled=True)
    pieces_list = []
    for offset_idx in range(col_ratio):
        pieces_list.append(spread(column_panel, "col", row_place * col_ratio + offset_idx))
    left_cols = jnp.concatenate(pieces_list, axis=1)
    selected = left_cols
    summed = jnp.einsum(
        "kic,kjc->ijc",
        selected,
        lax.all_gather(right, "row", axis=0, tiled=True),
        preferred_element_type=jnp.float32,
    )
    return finish(pair_mid, summed, gate, 1, norm_gain, norm_bias, w_out_q, exp_out)


def solution(mesh):
    placed = (P("row", "col", None), P(), P(), P(), P(), P(), P(), P())
    return jax.shard_map(
        shards, mesh=mesh, in_specs=placed, out_specs=P("row", "col", None), check_vma=False
    )
```

profile of v0, /device:TPU:0, one launch (start us, length us, event | category | flops | bytes accessed | tf_op | source)
XLA Modules:
  0.0 389.6 jit_solution(5334776976437683013)
XLA Ops:
  6.5 0.7 convert_element_type.115
  7.4 1.0 fusion.65
  8.5 0.2 copy.126
  8.6 0.7 exponential_bitcast_fusion.1
  9.3 0.1 copy.96
  9.5 0.1 reshape.147
  9.6 1.4 convert_reduce_fusion.1
  11.2 0.6 fusion.14
  12.1 1.0 fusion.44
  13.2 2.1 fusion.32
  15.2 0.6 copy-done
  15.9 0.7 all-gather.7.cloned.1.call-update
  16.7 39.4 %all-gather.5.cloned.1.call-done = bf16[64,256,128]{2,1,0:T(8,128)(2,1)} async-done(((bf16[64,32,128]{2,1,0:T(8,128)(2,1)}), bf16[64,256,128]{2,1,0:T(8,128)(2,1)}) %all-gather.5.cloned.1.call-update) | async-done | bytes 4194320 | tf_op jit(solution)/shard_map/all_gather | solution.py:72
  56.1 3.1 dynamic-slice_select_fusion
  59.3 0.8 copy-done.3
  60.0 0.1 copy.127
  60.2 0.1 copy.101
  60.3 0.1 reshape.148
  60.4 0.2 copy.128
  60.6 0.1 copy.109
  60.9 34.4 %all-gather.7.cloned.1.call-done = bf16[64,256,128]{2,1,0:T(8,128)(2,1)} async-done(((bf16[64,32,128]{2,1,0:T(8,128)(2,1)}), bf16[64,256,128]{2,1,0:T(8,128)(2,1)}) %all-gather.7.cloned.1.call-update) | async-done | bytes 4194320 | tf_op jit(solution)/shard_map/all_gather | solution.py:78
  95.4 15.6 %copy.99 = bf16[64,256,128]{0,1,2:T(8,128)(2,1)} copy(bf16[64,256,128]{2,1,0:T(8,128)(2,1)} %all-gather.7.cloned.1.call-done) | data formatting | bytes 8388608 | tf_op jit(solution)/shard_map/all_gather | solution.py:78
  111.0 72.9 %all-reduce.4.cloned.1.call-done = bf16[32,256,128]{2,1,0:T(8,128)(2,1)} async-done(((bf16[32,256,128]{2,1,0:T(8,128)(2,1)}), bf16[32,256,128]{2,1,0:T(8,128)(2,1)}) %all-reduce.4.cloned.1.call-update) | async-done | bytes 2097168 | tf_op jit(solution)/shard_map/psum | solution.py:11
  183.9 3.4 copy.98
  187.3 4.8 %bitcast_reduce_fusion.1 = (f32[64,32]{0,1:T(8,128)S(1)}, f32[128,32,64]{2,1,0:T(8,128)S(1)}) fusion(bf16[32,256,128]{1,0,2:T(8,128)(2,1)S(1)} %copy.98, bf16[64,256,128]{0,1,2:T(8,128)(2,1)} %copy.99), kind=kOutput, calls=%fused_computation.7 | convolution fusion | flops 134477824 | bytes 7348224 | tf_op jit(solution)/shard_map/ikc,jkc->ijc/dot_general | solution.py:76
  192.1 0.3 multiply_reduce_fusion.1
  192.5 0.4 add_convert_fusion.1
  192.9 1.5 copy.102
  194.5 1.8 convert_reduce_fusion
  196.4 0.6 fusion.10
  197.2 1.0 fusion.46
  198.3 2.0 fusion.19
  200.2 0.7 copy-done.1
  201.0 0.5 all-gather.9.cloned.1.call-update
  201.5 0.2 all-reduce.6.cloned.1.call-start
  201.7 44.0 %all-gather.11.cloned.1.call-done = bf16[256,32,128]{2,1,0:T(8,128)(2,1)} async-done(((bf16[64,32,128]{2,1,0:T(8,128)(2,1)}), bf16[256,32,128]{2,1,0:T(8,128)(2,1)}) %all-gather.11.cloned.1.call-update) | async-done | bytes 2097168 | tf_op jit(solution)/shard_map/all_gather | solution.py:86
  245.8 3.9 %copy.111 = bf16[256,32,128]{0,1,2:T(8,128)(2,1)S(1)} copy(bf16[256,32,128]{2,1,0:T(8,128)(2,1)} %all-gather.11.cloned.1.call-done) | data formatting | bytes 4194304 | tf_op jit(solution)/shard_map/all_gather | solution.py:86
  249.7 2.3 broadcast_select_fusion.1
  252.0 0.1 copy.129
  252.1 0.1 copy.115
  252.4 39.3 %all-gather.9.cloned.1.call-done = bf16[256,32,128]{2,1,0:T(8,128)(2,1)} async-done(((bf16[64,32,128]{2,1,0:T(8,128)(2,1)}), bf16[256,32,128]{2,1,0:T(8,128)(2,1)}) %all-gather.9.cloned.1.call-update) | async-done | bytes 2097168 | tf_op jit(solution)/shard_map/all_gather | solution.py:95
  291.7 3.9 %copy.113 = bf16[256,32,128]{0,1,2:T(8,128)(2,1)S(1)} copy(bf16[256,32,128]{2,1,0:T(8,128)(2,1)} %all-gather.9.cloned.1.call-done) | data formatting | bytes 4194304 | tf_op jit(solution)/shard_map/all_gather | solution.py:95
  295.6 78.9 %all-reduce.6.cloned.1.call-done = (bf16[256,32,128]{0,1,2:T(8,128)(2,1)}, bf16[256,32,128]{0,1,2:T(8,128)(2,1)}) async-done(((bf16[256,32,128]{0,1,2:T(8,128)(2,1)}, bf16[256,32,128]{0,1,2:T(8,128)(2,1)}), (bf16[256,32,128]{0,1,2:T(8,128)(2,1)}, bf16[256,32,128]{0,1,2:T(8,128)(2,1)})) %all-reduce.6.cloned.1.call-update) | async-done | bytes 4194320 | tf_op jit(solution)/shard_map/psum | solution.py:11
  374.5 3.4 bitcast_reduce_fusion
  378.0 0.3 multiply_reduce_fusion
  378.3 0.4 add_convert_fusion
  378.7 1.5 copy.116
  380.3 2.4 fusion.5
  (52 shorter events, 1.8 us)
Async XLA Ops:
  6.5 4.6 %copy-start.2 = (bf16[64,32,128]{2,1,0:T(8,128)(2,1)S(1)}, bf16[64,32,128]{2,1,0:T(8,128)(2,1)}, u32[]{:S(2)}) copy-start(bf16[64,32,128]{2,1,0:T(8,128)(2,1)} %param.8) | copy-start | bytes 1572868
  6.5 5.5 %copy-start.6 = (f32[2,2,128]{2,1,0:T(2,128)S(1)}, f32[2,2,128]{2,1,0:T(2,128)}, u32[]{:S(2)}) copy-start(f32[2,2,128]{2,1,0:T(2,128)} %param.10) | copy-start | bytes 6148
  6.5 5.5 %copy-start.5 = (f32[2,2,128]{2,1,0:T(2,128)S(1)}, f32[2,2,128]{2,1,0:T(2,128)}, u32[]{:S(2)}) copy-start(f32[2,2,128]{2,1,0:T(2,128)} %param.11) | copy-start | bytes 6148
  6.5 49.6 %all-gather.5.cloned.1.call-start = ((), (), s32[]{:S(2)}) async-start(), calls=%async_computation | async-start | bytes 4718592 | tf_op jit(solution)/shard_map/all_gather | solution.py:72
  13.2 2.7 copy-start
  15.9 79.5 %all-gather.7.cloned.1.call-start = ((), (), s32[]{:S(2)}) async-start(), calls=%async_computation.2 | async-start | bytes 4718592 | tf_op jit(solution)/shard_map/all_gather | solution.py:78
  16.7 167.3 %all-reduce.4.cloned.1.call-start = ((), (), s32[]{:S(2)}) async-start(), calls=%async_computation.1 | async-start | bytes 4194304 | tf_op jit(solution)/shard_map/psum | solution.py:11
  59.2 0.8 copy-start.3
  59.2 1.0 copy-start.4
  59.2 186.6 %all-gather.11.cloned.1.call-start = ((), (), s32[]{:S(2)}) async-start(), calls=%async_computation.4 | async-start | bytes 2621440 | tf_op jit(solution)/shard_map/all_gather | solution.py:86
  198.2 2.6 copy-start.1
  200.9 90.8 %all-gather.9.cloned.1.call-start = ((), (), s32[]{:S(2)}) async-start(), calls=%async_computation.3 | async-start | bytes 2621440 | tf_op jit(solution)/shard_map/all_gather | solution.py:95
  201.5 173.0 %all-reduce.6.cloned.1.call-start = ((), (), s32[]{:S(2)}) async-start(), calls=%async_computation.5 | async-start | bytes 8388608 | tf_op jit(solution)/shard_map/psum | solution.py:11
Sparse Core Ops, SparseCore 0:
  16.0 40.0 all-gather.4
  58.0 37.3 all-gather.6
  97.7 86.1 all-reduce.3
  201.0 44.6 all-gather.10
  247.2 44.4 all-gather.8
  294.8 79.6 all-reduce.5
where the time goes:
time: 390 us
  waiting for transfers between devices  310 us (79%)
  local copies, waits for them, and re-layouts  35.4 us (9%)
  other arithmetic  15.3 us (4%)
  matrix products  14.5 us (4%)
  between operations  13.8 us (4%)
    psum x2, waiting for transfers between devices, spread(): return lax.psum(jnp.where(mine, x, jnp.zeros_like(x)), axis)  152 us
    all_gather x1, waiting for transfers between devices, shards(): column_panel = lax.all_gather(left, 'row', axis=0, tiled=True)  44 us
    all_gather x1, waiting for transfers between devices, shards(): right_panel = lax.all_gather(right, 'col', axis=1, tiled=True)  39.4 us
    all_gather x1, waiting for transfers between devices, shards(): lax.all_gather(right, 'row', axis=0, tiled=True)  39.3 us
    all_gather x1, waiting for transfers between devices, shards(): lax.all_gather(left, 'col', axis=1, tiled=True)  34.4 us
    all_gather x1, local copies, waits for them, and re-layouts, shards(): lax.all_gather(left, 'col', axis=1, tiled=True)  15.6 us
  transfers between devices with their start and end apart: 6, of which 6 were waited for; matrix products, arithmetic and copies ran while one was open for 8% of the time, Pallas kernels for 0%

commit v1 on v0

v1 whole, which is shorter than its diff:
```python
import functools

import jax
import jax.numpy as jnp
from jax import lax
from jax.experimental import pallas as pl
from jax.experimental.pallas import tpu as pltpu
from jax.sharding import PartitionSpec as P

BLK = 32
AXES = ("row", "col")
EPS = 1e-05


def layer_norm(values, scale_vec, shift_vec):
    average = jnp.mean(values, axis=-1, keepdims=True)
    centred = values - average
    variance = jnp.mean(centred * centred, axis=-1, keepdims=True)
    return centred * lax.rsqrt(variance + EPS) * scale_vec + shift_vec


def dequantize(quantized, exponents, block_size):
    scales = jnp.exp2(exponents.astype(jnp.float32))
    scales = jnp.repeat(jnp.repeat(scales, block_size, axis=0), block_size, axis=1)
    return (quantized.astype(jnp.float32) * scales).astype(jnp.bfloat16)


def plain_update(layer, pair, row_mask, col_mask, norm_gain, norm_bias, w_in, w_out):
    rows_n, cols_n, width = pair.shape
    row_count, col_count = lax.axis_size("row"), lax.axis_size("col")
    parts = row_count * col_count
    own = width // parts
    normed = layer_norm(
        pair.astype(jnp.float32), norm_gain[layer, 0], norm_bias[layer, 0]
    ).astype(jnp.bfloat16)
    proj = jnp.einsum("ijc,cd->ijd", normed, w_in, preferred_element_type=jnp.float32)
    p0, p1, p2, p3, p4 = jnp.split(proj, 5, axis=-1)
    pm = (row_mask[:, None] * col_mask[None, :])[:, :, None]
    left = (jax.nn.sigmoid(p0) * p1 * pm).astype(jnp.bfloat16)
    right = (jax.nn.sigmoid(p2) * p3 * pm).astype(jnp.bfloat16)
    sent = jnp.stack([left, right]).reshape(2, rows_n, cols_n, parts, own)
    got = lax.all_to_all(sent.transpose(3, 0, 4, 1, 2), AXES, 0, 0, tiled=True)
    got = got.reshape(row_count, col_count, 2, own, rows_n, cols_n)
    whole = got.transpose(2, 3, 0, 4, 1, 5).reshape(
        2, own, row_count * rows_n, col_count * cols_n
    )
    spec = "cik,cjk->cij" if layer == 0 else "cki,ckj->cij"
    x = jnp.einsum(spec, whole[0], whole[1], preferred_element_type=jnp.float32)
    x = x.astype(jnp.bfloat16).reshape(own, row_count, rows_n, col_count, cols_n)
    back = x.transpose(1, 3, 0, 2, 4).reshape(parts, own, rows_n, cols_n)
    back = lax.all_to_all(back, AXES, 0, 0, tiled=True)
    x = back.transpose(2, 3, 0, 1).reshape(rows_n, cols_n, width)
    y = layer_norm(
        x.astype(jnp.float32), norm_gain[layer, 1], norm_bias[layer, 1]
    ).astype(jnp.bfloat16)
    out = jnp.einsum("ijc,cd->ijd", y, w_out, preferred_element_type=jnp.float32)
    return (pair.astype(jnp.float32) + jax.nn.sigmoid(p4) * out).astype(jnp.bfloat16)


def plain(pair, residue_mask, norm_gain, norm_bias, w_in_q, exp_in, w_out_q, exp_out):
    rows_n, cols_n, _ = pair.shape
    mask = residue_mask.astype(jnp.float32)
    row_mask = lax.dynamic_slice_in_dim(mask, lax.axis_index("row") * rows_n, rows_n)
    col_mask = lax.dynamic_slice_in_dim(mask, lax.axis_index("col") * cols_n, cols_n)
    for layer in range(2):
        w_in = dequantize(w_in_q[layer], exp_in[layer], BLK)
        w_out = dequantize(w_out_q[layer], exp_out[layer], BLK)
        pair = plain_update(
            layer, pair, row_mask, col_mask, norm_gain, norm_bias, w_in, w_out
        )
    return pair


PACK = 16


def swap_lanes(values):
    size = len(values)
    lanes = values[0].shape[-1]
    lane = lax.broadcasted_iota(jnp.int32, values[0].shape, 1)
    step = 1
    while step < size:
        low = (lane & step) == 0
        made = list(values)
        for v in range(size):
            if v & step == 0:
                a, b = values[v], values[v | step]
                made[v] = jnp.where(low, a, pltpu.roll(b, step, 1))
                made[v | step] = jnp.where(low, pltpu.roll(a, lanes - step, 1), b)
        values = made
        step *= 2
    return values


def norm_rows(values, gain, bias):
    average = jnp.mean(values, axis=-1, keepdims=True)
    centred = values - average
    variance = jnp.mean(centred * centred, axis=-1, keepdims=True)
    return (centred * lax.rsqrt(variance + EPS) * gain + bias).astype(jnp.bfloat16)


def scaled(q_ref, exp_ref, layer, first, count):
    width = q_ref.shape[1]
    per = 128 // BLK
    block = lax.broadcasted_iota(jnp.int32, (1, 128), 1) // BLK
    tiles = []
    for t in range(first, first + count):
        rows = []
        for rb in range(width // BLK):
            e = jnp.zeros((1, 128), jnp.int32)
            for s in range(per):
                e = jnp.where(block == s, exp_ref[layer, rb, t * per + s], e)
            q = q_ref[layer, rb * BLK : (rb + 1) * BLK, t * 128 : (t + 1) * 128]
            scale = jnp.exp2(e.astype(jnp.float32))
            rows.append((q.astype(jnp.float32) * scale).astype(jnp.bfloat16))
        tiles.append(jnp.concatenate(rows, axis=0))
    return jnp.concatenate(tiles, axis=1)


def gated(normed, weights, width):
    proj = jnp.dot(normed, weights, preferred_element_type=jnp.float32)
    p0, p1, p2, p3 = (proj[:, t * width : (t + 1) * width] for t in range(4))
    left = (jax.nn.sigmoid(p0) * p1).astype(jnp.bfloat16)
    right = (jax.nn.sigmoid(p2) * p3).astype(jnp.bfloat16)
    return left, right


def scatter_lanes(l_ref, r_ref, send_ref):
    size = send_ref.shape[0]
    outer = l_ref.shape[0] // size
    rows = l_ref.shape[1]
    for side, ref in enumerate((l_ref, r_ref)):
        for o in range(outer):
            for b in range(0, rows, PACK):
                got = swap_lanes([ref[o * size + v, b : b + PACK, :] for v in range(size)])
                at = (side * outer + o) * rows + b
                for d in range(size):
                    send_ref[d, at : at + PACK, :] = got[d]


def open_kernel(pair_ref, gain_ref, bias_ref, q_ref, exp_ref, send_ref, t_ref, l_ref, r_ref):
    rows_n, cols_n, width = pair_ref.shape
    weights = scaled(q_ref, exp_ref, 0, 0, 4)
    gain, bias = gain_ref[0, 0:1, :], bias_ref[0, 0:1, :]
    t_ref[...] = pair_ref[...].astype(jnp.float32)
    step = 8
    for k in range(0, cols_n, step):
        part = jnp.concatenate([t_ref[:, k + s, :] for s in range(step)], axis=0)
        left, right = gated(norm_rows(part, gain, bias), weights, width)
        l_ref[k : k + step] = left.reshape(step, rows_n, width)
        r_ref[k : k + step] = right.reshape(step, rows_n, width)
    scatter_lanes(l_ref, r_ref, send_ref)


def gate_kernel(layer, pair_ref, gain_ref, bias_ref, q_ref, exp_ref, gate_ref):
    rows_n, cols_n, width = pair_ref.shape
    weights = scaled(q_ref, exp_ref, layer, 4, 1)
    gain, bias = gain_ref[layer, 0:1, :], bias_ref[layer, 0:1, :]
    step = 16
    for i in range(0, rows_n, step):
        part = pair_ref[i : i + step].astype(jnp.float32).reshape(step * cols_n, width)
        proj = jnp.dot(
            norm_rows(part, gain, bias), weights, preferred_element_type=jnp.float32
        )
        gate_ref[i : i + step] = jax.nn.sigmoid(proj).reshape(step, cols_n, width)


def product_kernel(layer, row_count, own, got_ref, lane_ref, row_ref, x_ref):
    parts, both, lanes = got_ref.shape
    rows = both // 2
    col_count = parts // row_count
    size = lanes // own
    outer = rows // size
    tiles = lane_ref.shape[0]

    def tile(side, block, t):
        if layer == 0:
            r, h, c = block // outer, block % outer, t
        else:
            r, h, c = t // outer, t % outer, block
        at = side * rows + h * size
        return got_ref[r * col_count + c, at : at + size, :]

    group = lax.broadcasted_iota(jnp.int32, (1, lanes), 1) // size
    masks = [
        [jnp.where(group == a, lane_ref[t : t + 1, :], 0.0).astype(jnp.bfloat16) for t in range(tiles)]
        for a in range(own)
    ]
    right = jnp.concatenate(
        [
            jnp.concatenate([tile(1, block, t) for t in range(tiles)], axis=1)
            for block in range(tiles)
        ],
        axis=0,
    )
    for r in range(row_count):
        spread = []
        for h in range(outer):
            mine = [tile(0, r * outer + h, t) for t in range(tiles)]
            for a in range(own):
                spread.append(
                    jnp.concatenate([mine[t] * masks[a][t] for t in range(tiles)], axis=1)
                )
        left = jnp.concatenate(spread, axis=0)
        x = lax.dot_general(
            right, left, (((1,), (1,)), ((), ())), preferred_element_type=jnp.float32
        )
        for h in range(outer):
            block = r * outer + h
            piece = x[:, h * lanes : (h + 1) * lanes]
            piece = (piece * row_ref[...] * lane_ref[block : block + 1, :]).astype(jnp.bfloat16)
            for c in range(col_count):
                x_ref[r * col_count + c, h * size : (h + 1) * size, :] = piece[
                    c * size : (c + 1) * size, :
                ]


def gather_lanes(x_ref, u_ref):
    size = x_ref.shape[0]
    cols = u_ref.shape[1]
    outer = u_ref.shape[0] // size
    for o in range(outer):
        for b in range(0, cols, PACK):
            at = o * cols + b
            got = swap_lanes([x_ref[d, at : at + PACK, :] for d in range(size)])
            for v in range(size):
                u_ref[o * size + v, b : b + PACK, :] = got[v]


def finish_rows(layer, at, step, u_ref, pair_ref, gate_ref, gain_ref, bias_ref, w_out):
    _, cols_n, width = pair_ref.shape
    flat = (step * cols_n, width)
    x = u_ref[at : at + step].astype(jnp.float32).reshape(flat)
    y = norm_rows(x, gain_ref[layer, 1:2, :], bias_ref[layer, 1:2, :])
    update = jnp.dot(y, w_out, preferred_element_type=jnp.float32)
    base = pair_ref[at : at + step].astype(jnp.float32).reshape(flat)
    return (base + gate_ref[at : at + step].reshape(flat) * update).astype(jnp.bfloat16)


def middle_kernel(
    x_ref, pair_ref, gate_ref, gain_ref, bias_ref, q_ref, exp_ref, o_ref, oexp_ref,
    mid_ref, send_ref, u_ref, l_ref, r_ref,
):
    rows_n, cols_n, width = pair_ref.shape
    w_out = scaled(o_ref, oexp_ref, 0, 0, 1)
    weights = scaled(q_ref, exp_ref, 1, 0, 4)
    gain, bias = gain_ref[1, 0:1, :], bias_ref[1, 0:1, :]
    gather_lanes(x_ref, u_ref)
    step = 16
    for i in range(0, rows_n, step):
        mid = finish_rows(0, i, step, u_ref, pair_ref, gate_ref, gain_ref, bias_ref, w_out)
        mid_ref[i : i + step] = mid.reshape(step, cols_n, width)
        left, right = gated(norm_rows(mid.astype(jnp.float32), gain, bias), weights, width)
        l_ref[i : i + step] = left.reshape(step, cols_n, width)
        r_ref[i : i + step] = right.reshape(step, cols_n, width)
    scatter_lanes(l_ref, r_ref, send_ref)


def close_kernel(
    x_ref, pair_ref, gate_ref, gain_ref, bias_ref, o_ref, oexp_ref, out_ref, u_ref
):
    rows_n, cols_n, width = pair_ref.shape
    w_out = scaled(o_ref, oexp_ref, 1, 0, 1)
    gather_lanes(x_ref, u_ref)
    step = 16
    for i in range(0, rows_n, step):
        out = finish_rows(1, i, step, u_ref, pair_ref, gate_ref, gain_ref, bias_ref, w_out)
        out_ref[i : i + step] = out.reshape(step, cols_n, width)


VMEM = pl.BlockSpec(memory_space=pltpu.VMEM)
SMEM = pl.BlockSpec(memory_space=pltpu.SMEM)


def call(body, name, specs, outs, scratch, flops, moved):
    return pl.pallas_call(
        body,
        name=name,
        in_specs=specs,
        out_specs=jax.tree.map(lambda _: VMEM, outs),
        out_shape=outs,
        scratch_shapes=scratch,
        cost_estimate=pl.CostEstimate(flops=flops, bytes_accessed=moved, transcendentals=0),
        compiler_params=pltpu.CompilerParams(vmem_limit_bytes=40 * 2**20),
    )


def fast(pair, residue_mask, norm_gain, norm_bias, w_in_q, exp_in, w_out_q, exp_out):
    rows_n, cols_n, width = pair.shape
    row_count, col_count = lax.axis_size("row"), lax.axis_size("col")
    parts = row_count * col_count
    own = width // parts
    tokens = residue_mask.shape[0]
    bf16, f32 = jnp.bfloat16, jnp.float32
    mask = residue_mask.astype(f32)
    lane_mask = jnp.tile(mask.reshape(tokens // cols_n, cols_n), (1, own))
    row_mask = jnp.broadcast_to(mask[:, None], (tokens, width))

    block = (rows_n, cols_n, width)
    sent = jax.ShapeDtypeStruct((parts, 2 * rows_n, width), bf16)
    back = jax.ShapeDtypeStruct((parts, rows_n, width), bf16)
    pairs = rows_n * cols_n
    proj_cost = (2 * pairs * width * 4 * width, 8 * pairs * width)
    side = pltpu.VMEM(block, bf16)
    gate_out = jax.ShapeDtypeStruct(block, f32)

    def gate(layer, source):
        return call(
            functools.partial(gate_kernel, layer), f"gate{layer}",
            [VMEM, VMEM, VMEM, VMEM, SMEM], gate_out, [],
            2 * pairs * width * width, 8 * pairs * width,
        )(source, norm_gain, norm_bias, w_in_q, exp_in)

    def product(layer, got):
        return call(
            functools.partial(product_kernel, layer, row_count, own), f"product{layer}",
            [VMEM, VMEM, VMEM], back, [],
            2 * tokens * tokens * tokens * own * own, 6 * pairs * width,
        )(got, lane_mask, row_mask)

    def exchange(x):
        return lax.all_to_all(x, AXES, 0, 0, tiled=True)

    turned = pltpu.VMEM((cols_n, rows_n, width), bf16)
    send = call(
        open_kernel, "open", [VMEM, VMEM, VMEM, VMEM, SMEM], sent,
        [pltpu.VMEM(block, f32), turned, turned], *proj_cost,
    )(pair, norm_gain, norm_bias, w_in_q, exp_in)
    got = exchange(send)
    gate0 = gate(0, pair)
    x = exchange(product(0, got))
    mid, send = call(
        middle_kernel, "middle", [VMEM] * 6 + [SMEM, VMEM, SMEM],
        (jax.ShapeDtypeStruct(block, bf16), sent), [side, side, side], *proj_cost,
    )(x, pair, gate0, norm_gain, norm_bias, w_in_q, exp_in, w_out_q, exp_out)
    got = exchange(send)
    gate1 = gate(1, mid)
    x = exchange(product(1, got))
    return call(
        close_kernel, "close", [VMEM] * 6 + [SMEM],
        jax.ShapeDtypeStruct(block, bf16), [side], *proj_cost,
    )(x, mid, gate1, norm_gain, norm_bias, w_out_q, exp_out)


def solution(mesh):
    parts = mesh.shape["row"] * mesh.shape["col"]

    def shards(pair, *rest):
        rows_n, cols_n, width = pair.shape
        fits = (
            width == 128
            and width % parts == 0
            and cols_n == parts
            and rows_n % cols_n == 0
            and cols_n % PACK == 0
        )
        return (fast if fits else plain)(pair, *rest)

    placed = (P("row", "col", None), P(), P(), P(), P(), P(), P(), P())
    return jax.shard_map(
        shards, mesh=mesh, in_specs=placed, out_specs=P("row", "col", None), check_vma=False
    )
```

time: 390 us -> 125 us (0.32)
  waiting for transfers between devices: 310 us -> 54.4 us
  local copies, waits for them, and re-layouts: 35.4 us -> 4.35 us
  blocking collectives: 0 us -> 29 us
  Pallas kernels: 0 us -> 21.7 us
  other arithmetic: 15.3 us -> 0.01 us
  matrix products: 14.5 us -> 0 us
  starting transfers between devices: 0.38 us -> 14.6 us
  between operations: 13.8 us -> 0.15 us
    all_gather x4 -> x0, waiting for transfers between devices: 157 us -> none  [the longest x1 44 us: shards(): column_panel = lax.all_gather(left, 'row', axis=0, tiled=True)]
    psum x2 -> x0, waiting for transfers between devices: 152 us -> none  [spread(): return lax.psum(jnp.where(mine, x, jnp.zeros_like(x)), axis)]
    all_to_all x0 -> x3, waiting for transfers between devices: none -> 54.4 us  [exchange(): return lax.all_to_all(x, AXES, 0, 0, tiled=True)]
    all_to_all x0 -> x1, blocking collectives: none -> 29 us  [exchange(): return lax.all_to_all(x, AXES, 0, 0, tiled=True)]
    all_gather x3 -> x0, local copies, waits for them, and re-layouts: 23.5 us -> none  [the longest x1 15.6 us: shards(): lax.all_gather(left, 'col', axis=1, tiled=True)]
    pallas_call x0 -> x7, Pallas kernels: none -> 21.7 us  [the longest x1 6.53 us: fast(): call(middle_kernel, 'middle', [VMEM] * 6 + [SMEM, VMEM, SMEM], (jax.Shape...]
    all_to_all x0 -> x3, starting transfers between devices: none -> 14.6 us  [exchange(): return lax.all_to_all(x, AXES, 0, 0, tiled=True)]
    dot_general x6 -> x0, matrix products: 14.5 us -> none  [the longest x1 4.79 us: shards(): jnp.einsum('ikc,jkc->ijc', lax.all_gather(left, 'col', axis=1, tiled=True...]
  transfers between devices with their start and end apart: 6 -> 3, of which waited for: 6 -> 3; matrix products, arithmetic and copies ran while one was open for 8% -> 0% of each run, Pallas kernels for 0% -> 2%
where the time goes in v1:
time: 125 us; the launch traced here: 124 us
  waiting for transfers between devices  54.4 us (44%)
  blocking collectives  29 us (23%)
  Pallas kernels  21.7 us (17%)
  starting transfers between devices  14.6 us (12%)
  local copies, waits for them, and re-layouts  4.35 us (3%)
    all_to_all x3, waiting for transfers between devices, exchange(): return lax.all_to_all(x, AXES, 0, 0, tiled=True)  54.4 us
    all_to_all x1, blocking collectives, exchange(): return lax.all_to_all(x, AXES, 0, 0, tiled=True)  29 us
    all_to_all x3, starting transfers between devices, exchange(): return lax.all_to_all(x, AXES, 0, 0, tiled=True)  14.6 us
    pallas_call x1, Pallas kernels, fast(): call(middle_kernel, 'middle', [VMEM] * 6 + [SMEM, VMEM, SMEM], (jax.Shape...  6.53 us
    pallas_call x1, Pallas kernels, fast(): call(open_kernel, 'open', [VMEM, VMEM, VMEM, VMEM, SMEM], sent, [pltpu.VM...  5.89 us
    unnamed x26, local copies, waits for them, and re-layouts  4.1 us
    pallas_call x1, Pallas kernels, fast(): call(close_kernel, 'close', [VMEM] * 6 + [SMEM], jax.ShapeDtypeStruct(blo...  3.44 us
    pallas_call x2, Pallas kernels, product(): call(functools.partial(product_kernel, layer, row_count, own), f'product{...  3.12 us
  transfers between devices with their start and end apart: 3, of which 3 were waited for; matrix products, arithmetic and copies ran while one was open for 0% of the time, Pallas kernels for 2%

profile of v1, /device:TPU:0, one launch (start us, length us, event | category | flops | bytes accessed | tf_op | source)
XLA Modules:
  0.0 124.2 jit_solution(3180436676929426397)
XLA Ops:
  0.0 0.0 copy-start
  0.0 1.0 copy-done
  1.0 0.0 copy-start.2
  1.0 1.0 copy-done.2
  2.0 0.0 copy-start.5
  2.0 0.7 copy-done.5
  2.7 0.0 copy-start.7
  2.7 0.7 copy-done.7
  3.4 0.0 copy-start.9
  3.4 0.7 copy-done.9
  4.1 5.9 %open.1 = bf16[32,128,128]{2,1,0:T(8,128)(2,1)} custom-call(bf16[64,32,128]{2,1,0:T(8,128)(2,1)S(1)} %copy-done.2, f32[2,2,128]{2,1,0:T(2,128)S(1)} %copy-done.7, f32[2,2,128]{2,1,0:T(2,128)S(1)} %copy-done.9, bf16[2,128,640]{2,1,0:T(8,128)(2,1)S(1)} %copy-done, s32[2,4,20]{2,1,0:T(4,128)S(1)} %copy-done.5), custom_call_target="tpu_custom_call" | custom-call | flops 268435456 | bytes 2097152 | tf_op jit(solution)/shard_map/open/pallas_call | solution.py:325
  10.0 0.0 copy-start.12
  10.0 7.3 %all-to-all-start = ((bf16[32,128,128]{2,1,0:T(8,128)(2,1)}), bf16[32,128,128]{2,1,0:T(8,128)(2,1)S(1)}, u32[]{:S(2)}, u32[]{:S(2)}) async-start(bf16[32,128,128]{2,1,0:T(8,128)(2,1)} %open.1), calls=%async_computation | async-start | bytes 2097152 | tf_op jit(solution)/shard_map/all_to_all | solution.py:322
  17.3 0.0 copy-done.12
  17.3 0.1 tile.10
  17.4 0.1 tile.12.lane_ref
  17.5 26.0 %all-to-all-done.got_ref = bf16[32,128,128]{2,1,0:T(8,128)(2,1)S(1)} async-done(((bf16[32,128,128]{2,1,0:T(8,128)(2,1)}), bf16[32,128,128]{2,1,0:T(8,128)(2,1)S(1)}, u32[]{:S(2)}, u32[]{:S(2)}) %all-to-all-start) | async-done | bytes 1048608 | tf_op jit(solution)/shard_map/all_to_all | solution.py:322
  43.5 0.1 broadcast_in_dim.2.row_ref
  43.6 1.6 %product0.1 = bf16[32,64,128]{2,1,0:T(8,128)(2,1)} custom-call(bf16[32,128,128]{2,1,0:T(8,128)(2,1)S(1)} %all-to-all-done.got_ref, f32[8,128]{1,0:T(8,128)S(1)} %tile.12.lane_ref, f32[256,128]{1,0:T(8,128)S(1)} %broadcast_in_dim.2.row_ref), custom_call_target="tpu_custom_call" | custom-call | flops 536870912 | bytes 1572864 | tf_op jit(solution)/shard_map/product0/pallas_call | solution.py:315
  45.1 0.0 copy-start.1
  45.1 0.0 copy-start.3
  45.1 0.0 copy-start.6
  45.2 0.0 copy-start.8
  45.2 0.0 copy-start.10
  45.2 3.6 %all-to-all-start.1 = ((bf16[32,64,128]{2,1,0:T(8,128)(2,1)}), bf16[32,64,128]{2,1,0:T(8,128)(2,1)S(1)}, u32[]{:S(2)}, u32[]{:S(2)}) async-start(bf16[32,64,128]{2,1,0:T(8,128)(2,1)} %product0.1), calls=%async_computation.1 | async-start | bytes 1048576 | tf_op jit(solution)/shard_map/all_to_all | solution.py:322
  48.8 0.0 copy-done.1
  48.8 0.0 copy-done.3
  48.8 0.0 copy-done.6
  48.8 0.0 copy-done.8
  48.8 0.0 copy-done.10
  48.9 0.0 copy-start.4
  48.9 0.0 copy-start.11
  48.9 1.4 %gate0.1.gate_ref = f32[64,32,128]{2,1,0:T(8,128)S(1)} custom-call(bf16[64,32,128]{2,1,0:T(8,128)(2,1)S(1)} %copy-done.3, f32[2,2,128]{2,1,0:T(2,128)S(1)} %copy-done.8, f32[2,2,128]{2,1,0:T(2,128)S(1)} %copy-done.10, bf16[2,128,640]{2,1,0:T(8,128)(2,1)S(1)} %copy-done.1, s32[2,4,20]{2,1,0:T(4,128)S(1)} %copy-done.6), custom_call_target="tpu_custom_call" | custom-call | flops 67108864 | bytes 2097152 | tf_op jit(solution)/shard_map/gate0/pallas_call | solution.py:308
  50.3 14.1 %all-to-all-done.1.x_ref = bf16[32,64,128]{2,1,0:T(8,128)(2,1)S(1)} async-done(((bf16[32,64,128]{2,1,0:T(8,128)(2,1)}), bf16[32,64,128]{2,1,0:T(8,128)(2,1)S(1)}, u32[]{:S(2)}, u32[]{:S(2)}) %all-to-all-start.1) | async-done | bytes 524320 | tf_op jit(solution)/shard_map/all_to_all | solution.py:322
  64.4 0.0 copy-done.4
  64.4 0.0 copy-done.11
  64.4 6.5 %middle.1 = (bf16[64,32,128]{2,1,0:T(8,128)(2,1)S(1)}, bf16[32,128,128]{2,1,0:T(8,128)(2,1)S(1)}) custom-call(bf16[32,64,128]{2,1,0:T(8,128)(2,1)S(1)} %all-to-all-done.1.x_ref, bf16[64,32,128]{2,1,0:T(8,128)(2,1)S(1)} %copy-done.3, f32[64,32,128]{2,1,0:T(8,128)S(1)} %gate0.1.gate_ref, f32[2,2,128]{2,1,0:T(2,128)S(1)} %copy-done.8, ...), custom_call_target="tpu_custom_call" | custom-call | flops 268435456 | bytes 2097152 | tf_op jit(solution)/shard_map/middle/pallas_call | solution.py:332
  71.0 29.0 %all_to_all.20.got_ref = bf16[32,128,128]{2,1,0:T(8,128)(2,1)S(1)} all-to-all(bf16[32,128,128]{2,1,0:T(8,128)(2,1)S(1)} %get-tuple-element.7), channel_id=1, replica_groups=mesh['row'=4,'col'=8] {'row','col'}, dimensions={0} | all-to-all | bytes 2097152 | tf_op jit(solution)/shard_map/all_to_all | solution.py:322
  100.0 1.6 %product1.1 = bf16[32,64,128]{2,1,0:T(8,128)(2,1)} custom-call(bf16[32,128,128]{2,1,0:T(8,128)(2,1)S(1)} %all_to_all.20.got_ref, f32[8,128]{1,0:T(8,128)S(1)} %tile.12.lane_ref, f32[256,128]{1,0:T(8,128)S(1)} %broadcast_in_dim.2.row_ref), custom_call_target="tpu_custom_call" | custom-call | flops 536870912 | bytes 1572864 | tf_op jit(solution)/shard_map/product1/pallas_call | solution.py:315
  101.5 3.6 %all-to-all-start.3 = ((bf16[32,64,128]{2,1,0:T(8,128)(2,1)}), bf16[32,64,128]{2,1,0:T(8,128)(2,1)S(1)}, u32[]{:S(2)}, u32[]{:S(2)}) async-start(bf16[32,64,128]{2,1,0:T(8,128)(2,1)} %product1.1), calls=%async_computation.3 | async-start | bytes 1048576 | tf_op jit(solution)/shard_map/all_to_all | solution.py:322
  105.1 1.4 %gate1.1.gate_ref = f32[64,32,128]{2,1,0:T(8,128)S(1)} custom-call(bf16[64,32,128]{2,1,0:T(8,128)(2,1)S(1)} %get-tuple-element.8.pair_ref, f32[2,2,128]{2,1,0:T(2,128)S(1)} %copy-done.8, f32[2,2,128]{2,1,0:T(2,128)S(1)} %copy-done.10, bf16[2,128,640]{2,1,0:T(8,128)(2,1)S(1)} %copy-done.1, s32[2,4,20]{2,1,0:T(4,128)S(1)} %copy-done.6), custom_call_target="tpu_custom_call" | custom-call | flops 67108864 | bytes 2097152 | tf_op jit(solution)/shard_map/gate1/pallas_call | solution.py:308
  106.5 14.2 %all-to-all-done.3.x_ref = bf16[32,64,128]{2,1,0:T(8,128)(2,1)S(1)} async-done(((bf16[32,64,128]{2,1,0:T(8,128)(2,1)}), bf16[32,64,128]{2,1,0:T(8,128)(2,1)S(1)}, u32[]{:S(2)}, u32[]{:S(2)}) %all-to-all-start.3) | async-done | bytes 524320 | tf_op jit(solution)/shard_map/all_to_all | solution.py:322
  120.8 3.4 %close.1 = bf16[64,32,128]{2,1,0:T(8,128)(2,1)} custom-call(bf16[32,64,128]{2,1,0:T(8,128)(2,1)S(1)} %all-to-all-done.3.x_ref, bf16[64,32,128]{2,1,0:T(8,128)(2,1)S(1)} %get-tuple-element.8.pair_ref, f32[64,32,128]{2,1,0:T(8,128)S(1)} %gate1.1.gate_ref, f32[2,2,128]{2,1,0:T(2,128)S(1)} %copy-done.8, f32[2,2,128]{2,1,0:T(2,128)S(1)} %copy-done.10, ...), custom_call_target="tpu_custom_call" | custom-call | flops 268435456 | bytes 2097152 | tf_op jit(solution)/shard_map/close/pallas_call | solution.py:339
  (2 shorter events, 0.0 us)
Async XLA Ops:
  0.0 1.0 copy-start
  1.0 1.0 copy-start.2
  2.0 0.7 copy-start.5
  2.7 0.7 copy-start.7
  3.4 0.7 copy-start.9
  10.0 7.3 %copy-start.12 = (s32[256]{0:T(256)S(1)}, s32[256]{0:T(256)}, u32[]{:S(2)}) copy-start(s32[256]{0:T(256)} %param.9) | copy-start | bytes 3076
  10.0 33.5 %all-to-all-start = ((bf16[32,128,128]{2,1,0:T(8,128)(2,1)}), bf16[32,128,128]{2,1,0:T(8,128)(2,1)S(1)}, u32[]{:S(2)}, u32[]{:S(2)}) async-start(bf16[32,128,128]{2,1,0:T(8,128)(2,1)} %open.1), calls=%async_computation | async-start | bytes 2097152 | tf_op jit(solution)/shard_map/all_to_all | solution.py:322
  45.1 3.7 %copy-start.1 = (bf16[2,128,640]{2,1,0:T(8,128)(2,1)S(1)}, bf16[2,128,640]{2,1,0:T(8,128)(2,1)}, u32[]{:S(2)}) copy-start(bf16[2,128,640]{2,1,0:T(8,128)(2,1)} %q_ref.7) | copy-start | bytes 983044
  45.1 3.7 %copy-start.3 = (bf16[64,32,128]{2,1,0:T(8,128)(2,1)S(1)}, bf16[64,32,128]{2,1,0:T(8,128)(2,1)}, u32[]{:S(2)}) copy-start(bf16[64,32,128]{2,1,0:T(8,128)(2,1)} %pair_ref.5) | copy-start | bytes 1572868
  45.1 3.7 %copy-start.6 = (s32[2,4,20]{2,1,0:T(4,128)S(1)}, s32[2,4,20]{2,1,0:T(4,128)}, u32[]{:S(2)}) copy-start(s32[2,4,20]{2,1,0:T(4,128)} %exp_ref.7) | copy-start | bytes 1924
  45.2 3.7 %copy-start.8 = (f32[2,2,128]{2,1,0:T(2,128)S(1)}, f32[2,2,128]{2,1,0:T(2,128)}, u32[]{:S(2)}) copy-start(f32[2,2,128]{2,1,0:T(2,128)} %gain_ref.9) | copy-start | bytes 6148
  45.2 3.7 %copy-start.10 = (f32[2,2,128]{2,1,0:T(2,128)S(1)}, f32[2,2,128]{2,1,0:T(2,128)}, u32[]{:S(2)}) copy-start(f32[2,2,128]{2,1,0:T(2,128)} %bias_ref.9) | copy-start | bytes 6148
  45.2 19.2 %all-to-all-start.1 = ((bf16[32,64,128]{2,1,0:T(8,128)(2,1)}), bf16[32,64,128]{2,1,0:T(8,128)(2,1)S(1)}, u32[]{:S(2)}, u32[]{:S(2)}) async-start(bf16[32,64,128]{2,1,0:T(8,128)(2,1)} %product0.1), calls=%async_computation.1 | async-start | bytes 1048576 | tf_op jit(solution)/shard_map/all_to_all | solution.py:322
  48.9 15.6 %copy-start.4 = (bf16[2,128,128]{2,1,0:T(8,128)(2,1)S(1)}, bf16[2,128,128]{2,1,0:T(8,128)(2,1)}, u32[]{:S(2)}) copy-start(bf16[2,128,128]{2,1,0:T(8,128)(2,1)} %o_ref.3) | copy-start | bytes 196612
  48.9 15.6 %copy-start.11 = (s32[2,4,4]{2,1,0:T(4,128)S(1)}, s32[2,4,4]{2,1,0:T(4,128)}, u32[]{:S(2)}) copy-start(s32[2,4,4]{2,1,0:T(4,128)} %oexp_ref.3) | copy-start | bytes 388
  101.5 19.2 %all-to-all-start.3 = ((bf16[32,64,128]{2,1,0:T(8,128)(2,1)}), bf16[32,64,128]{2,1,0:T(8,128)(2,1)S(1)}, u32[]{:S(2)}, u32[]{:S(2)}) async-start(bf16[32,64,128]{2,1,0:T(8,128)(2,1)} %product1.1), calls=%async_computation.3 | async-start | bytes 1048576 | tf_op jit(solution)/shard_map/all_to_all | solution.py:322

commit v2 on v1

--- a/solution.py
+++ b/solution.py
@@ -74,29 +74,73 @@
 PACK = 16
 
 
-def swap_lanes(values):
+def pick_lanes(values, slot, back=False):
     size = len(values)
-    lanes = values[0].shape[-1]
-    lane = lax.broadcasted_iota(jnp.int32, values[0].shape, 1)
+    lane = lax.broadcasted_iota(jnp.int32, values[0].shape, 1).astype(jnp.int16)
     step = 1
     while step < size:
-        low = (lane & step) == 0
-        made = list(values)
-        for v in range(size):
-            if v & step == 0:
-                a, b = values[v], values[v | step]
-                made[v] = jnp.where(low, a, pltpu.roll(b, step, 1))
-                made[v | step] = jnp.where(low, pltpu.roll(a, lanes - step, 1), b)
-        values = made
+        stay = (lane & jnp.int16(slot * step)) == 0
+        move = -step if back else step
+        values = [
+            jnp.where(stay, values[v], values[(v + move) % size]) for v in range(size)
+        ]
         step *= 2
     return values
 
 
+def turn_lanes(value, by, size):
+    if by == 0:
+        return value
+    lanes = value.shape[1]
+    lane = lax.broadcasted_iota(jnp.int32, value.shape, 1).astype(jnp.int16)
+    near = (lane & jnp.int16(size - 1)) < jnp.int16(size - by)
+    return jnp.where(
+        near, pltpu.roll(value, lanes - by, 1), pltpu.roll(value, size - by, 1)
+    )
+
+
+def twice(weights):
+    none = jnp.zeros_like(weights)
+    return jnp.concatenate(
+        [
+            jnp.concatenate([weights, none], axis=1),
+            jnp.concatenate([none, weights], axis=1),
+        ],
+        axis=0,
+    )
+
+
+def beside(rows):
+    half = rows.shape[0] // 2
+    return jnp.concatenate([rows[:half], rows[half:]], axis=1)
+
+
+def below(lanes):
+    half = lanes.shape[1] // 2
+    return jnp.concatenate([lanes[:, :half], lanes[:, half:]], axis=0)
+
+
+def norm_beside(values, gain, bias):
+    width = values.shape[1] // 2
+    share = jnp.full((width, width), 1.0 / width, jnp.float32)
+    row = lax.broadcasted_iota(jnp.int32, (width, width), 0)
+    column = lax.broadcasted_iota(jnp.int32, (width, width), 1)
+    centre = (row == column).astype(jnp.float32) - share
+    centred = jnp.dot(
+        values, twice(centre.astype(jnp.bfloat16)), preferred_element_type=jnp.float32
+    )
+    variance = jnp.dot(
+        (centred * centred).astype(jnp.bfloat16),
+        twice(share.astype(jnp.bfloat16)),
+        preferred_element_type=jnp.float32,
+    )
+    gain = jnp.concatenate([gain, gain], axis=1)
+    bias = jnp.concatenate([bias, bias], axis=1)
+    return (centred * lax.rsqrt(variance + EPS) * gain + bias).astype(jnp.bfloat16)
+
+
 def norm_rows(values, gain, bias):
-    average = jnp.mean(values, axis=-1, keepdims=True)
-    centred = values - average
-    variance = jnp.mean(centred * centred, axis=-1, keepdims=True)
-    return (centred * lax.rsqrt(variance + EPS) * gain + bias).astype(jnp.bfloat16)
+    return below(norm_beside(beside(values), gain, bias))
 
 
 def scaled(q_ref, exp_ref, layer, first, count):
@@ -117,12 +161,34 @@
     return jnp.concatenate(tiles, axis=1)
 
 
+def slotted(weights, width, size):
+    slot = width // size
+    row = lax.broadcasted_iota(jnp.int32, (width, width), 0)
+    column = lax.broadcasted_iota(jnp.int32, (width, width), 1)
+    order = (row == column % slot * size + column // slot).astype(jnp.bfloat16)
+    tiles = [
+        jnp.dot(
+            weights[:, t : t + width], order, preferred_element_type=jnp.float32
+        ).astype(jnp.bfloat16)
+        for t in range(0, weights.shape[1], width)
+    ]
+    return jnp.concatenate(tiles, axis=1)
+
+
 def gated(normed, weights, width):
     proj = jnp.dot(normed, weights, preferred_element_type=jnp.float32)
     p0, p1, p2, p3 = (proj[:, t * width : (t + 1) * width] for t in range(4))
-    left = (jax.nn.sigmoid(p0) * p1).astype(jnp.bfloat16)
-    right = (jax.nn.sigmoid(p2) * p3).astype(jnp.bfloat16)
-    return left, right
+    return jax.nn.sigmoid(p0) * p1, jax.nn.sigmoid(p2) * p3
+
+
+def put_rolled(ref, at, values, rows, size):
+    slot = values.shape[1] // size
+    for s in range(values.shape[0] // rows):
+        part = values[s * rows : (s + 1) * rows]
+        shift = (at + s) % size * slot
+        if shift:
+            part = pltpu.roll(part, shift, 1)
+        ref[at + s] = part.astype(jnp.bfloat16)
 
 
 def scatter_lanes(l_ref, r_ref, send_ref):
@@ -132,40 +198,68 @@
     for side, ref in enumerate((l_ref, r_ref)):
         for o in range(outer):
             for b in range(0, rows, PACK):
-                got = swap_lanes([ref[o * size + v, b : b + PACK, :] for v in range(size)])
+                got = pick_lanes(
+                    [ref[o * size + v, b : b + PACK, :] for v in range(size)],
+                    ref.shape[2] // size,
+                )
                 at = (side * outer + o) * rows + b
                 for d in range(size):
-                    send_ref[d, at : at + PACK, :] = got[d]
-
-
-def open_kernel(pair_ref, gain_ref, bias_ref, q_ref, exp_ref, send_ref, t_ref, l_ref, r_ref):
+                    send_ref[d, at : at + PACK, :] = got[-d % size]
+
+
+def open_kernel(
+    pair_hbm, gain_hbm, bias_hbm, q_hbm, exp_hbm, send_ref,
+    pair_ref, gain_ref, bias_ref, q_ref, exp_ref, t_ref, l_ref, r_ref, sems,
+):
+    moves = [
+        pltpu.make_async_copy(source, target, sems.at[n])
+        for n, (source, target) in enumerate(
+            (
+                (exp_hbm, exp_ref),
+                (q_hbm, q_ref),
+                (pair_hbm, pair_ref),
+                (gain_hbm, gain_ref),
+                (bias_hbm, bias_ref),
+            )
+        )
+    ]
+    for move in moves:
+        move.start()
+    for move in moves:
+        move.wait()
     rows_n, cols_n, width = pair_ref.shape
-    weights = scaled(q_ref, exp_ref, 0, 0, 4)
+    size = send_ref.shape[0]
+    weights = slotted(scaled(q_ref, exp_ref, 0, 0, 4), width, size)
     gain, bias = gain_ref[0, 0:1, :], bias_ref[0, 0:1, :]
-    t_ref[...] = pair_ref[...].astype(jnp.float32)
+    t_ref[...] = pair_ref[...].astype(jnp.float32).reshape(t_ref.shape)
     step = 8
     for k in range(0, cols_n, step):
-        part = jnp.concatenate([t_ref[:, k + s, :] for s in range(step)], axis=0)
+        part = jnp.concatenate(
+            [t_ref[pl.ds(k + s, rows_n, stride=cols_n), :] for s in range(step)], axis=0
+        )
+        part = part.astype(jnp.bfloat16)
         left, right = gated(norm_rows(part, gain, bias), weights, width)
-        l_ref[k : k + step] = left.reshape(step, rows_n, width)
-        r_ref[k : k + step] = right.reshape(step, rows_n, width)
+        put_rolled(l_ref, k, left, rows_n, size)
+        put_rolled(r_ref, k, right, rows_n, size)
     scatter_lanes(l_ref, r_ref, send_ref)
 
 
 def gate_kernel(layer, pair_ref, gain_ref, bias_ref, q_ref, exp_ref, gate_ref):
     rows_n, cols_n, width = pair_ref.shape
-    weights = scaled(q_ref, exp_ref, layer, 4, 1)
+    weights = twice(scaled(q_ref, exp_ref, layer, 4, 1))
     gain, bias = gain_ref[layer, 0:1, :], bias_ref[layer, 0:1, :]
     step = 16
     for i in range(0, rows_n, step):
-        part = pair_ref[i : i + step].astype(jnp.float32).reshape(step * cols_n, width)
+        part = beside(pair_ref[i : i + step].reshape(step * cols_n, width))
         proj = jnp.dot(
-            norm_rows(part, gain, bias), weights, preferred_element_type=jnp.float32
-        )
-        gate_ref[i : i + step] = jax.nn.sigmoid(proj).reshape(step, cols_n, width)
-
-
-def product_kernel(layer, row_count, own, got_ref, lane_ref, row_ref, x_ref):
+            norm_beside(part, gain, bias), weights, preferred_element_type=jnp.float32
+        )
+        gate_ref[i : i + step] = below(jax.nn.sigmoid(proj)).reshape(step, cols_n, width)
+
+
+def product_kernel(
+    layer, row_count, own, got_ref, sum_ref, lane_ref, row_ref, turn_ref, x_ref
+):
     parts, both, lanes = got_ref.shape
     rows = both // 2
     col_count = parts // row_count
@@ -181,9 +275,12 @@
         at = side * rows + h * size
         return got_ref[r * col_count + c, at : at + size, :]
 
-    group = lax.broadcasted_iota(jnp.int32, (1, lanes), 1) // size
+    channel = lax.broadcasted_iota(jnp.int32, (1, lanes), 1) % own
     masks = [
-        [jnp.where(group == a, lane_ref[t : t + 1, :], 0.0).astype(jnp.bfloat16) for t in range(tiles)]
+        [
+            jnp.where(channel == a, sum_ref[t : t + 1, :], 0.0).astype(jnp.bfloat16)
+            for t in range(tiles)
+        ]
         for a in range(own)
     ]
     right = jnp.concatenate(
@@ -208,7 +305,10 @@
         for h in range(outer):
             block = r * outer + h
             piece = x[:, h * lanes : (h + 1) * lanes]
-            piece = (piece * row_ref[...] * lane_ref[block : block + 1, :]).astype(jnp.bfloat16)
+            piece = piece * row_ref[...] * lane_ref[block : block + 1, :]
+            turn = jnp.broadcast_to(turn_ref[...], piece.shape)
+            piece = jnp.take_along_axis(piece, turn, axis=1, mode="promise_in_bounds")
+            piece = piece.astype(jnp.bfloat16)
             for c in range(col_count):
                 x_ref[r * col_count + c, h * size : (h + 1) * size, :] = piece[
                     c * size : (c + 1) * size, :
@@ -222,17 +322,19 @@
     for o in range(outer):
         for b in range(0, cols, PACK):
             at = o * cols + b
-            got = swap_lanes([x_ref[d, at : at + PACK, :] for d in range(size)])
+            got = pick_lanes(
+                [x_ref[-d % size, at : at + PACK, :] for d in range(size)], 1, True
+            )
             for v in range(size):
-                u_ref[o * size + v, b : b + PACK, :] = got[v]
+                u_ref[o * size + v, b : b + PACK, :] = turn_lanes(got[v], v, size)
 
 
 def finish_rows(layer, at, step, u_ref, pair_ref, gate_ref, gain_ref, bias_ref, w_out):
     _, cols_n, width = pair_ref.shape
     flat = (step * cols_n, width)
-    x = u_ref[at : at + step].astype(jnp.float32).reshape(flat)
-    y = norm_rows(x, gain_ref[layer, 1:2, :], bias_ref[layer, 1:2, :])
-    update = jnp.dot(y, w_out, preferred_element_type=jnp.float32)
+    x = beside(u_ref[at : at + step].reshape(flat))
+    y = norm_beside(x, gain_ref[layer, 1:2, :], bias_ref[layer, 1:2, :])
+    update = below(jnp.dot(y, w_out, preferred_element_type=jnp.float32))
     base = pair_ref[at : at + step].astype(jnp.float32).reshape(flat)
     return (base + gate_ref[at : at + step].reshape(flat) * update).astype(jnp.bfloat16)
 
@@ -242,17 +344,18 @@
     mid_ref, send_ref, u_ref, l_ref, r_ref,
 ):
     rows_n, cols_n, width = pair_ref.shape
-    w_out = scaled(o_ref, oexp_ref, 0, 0, 1)
-    weights = scaled(q_ref, exp_ref, 1, 0, 4)
+    w_out = twice(scaled(o_ref, oexp_ref, 0, 0, 1))
+    size = send_ref.shape[0]
+    weights = slotted(scaled(q_ref, exp_ref, 1, 0, 4), width, size)
     gain, bias = gain_ref[1, 0:1, :], bias_ref[1, 0:1, :]
     gather_lanes(x_ref, u_ref)
     step = 16
     for i in range(0, rows_n, step):
         mid = finish_rows(0, i, step, u_ref, pair_ref, gate_ref, gain_ref, bias_ref, w_out)
         mid_ref[i : i + step] = mid.reshape(step, cols_n, width)
-        left, right = gated(norm_rows(mid.astype(jnp.float32), gain, bias), weights, width)
-        l_ref[i : i + step] = left.reshape(step, cols_n, width)
-        r_ref[i : i + step] = right.reshape(step, cols_n, width)
+        left, right = gated(norm_rows(mid, gain, bias), weights, width)
+        put_rolled(l_ref, i, left, cols_n, size)
+        put_rolled(r_ref, i, right, cols_n, size)
     scatter_lanes(l_ref, r_ref, send_ref)
 
 
@@ -260,7 +363,7 @@
     x_ref, pair_ref, gate_ref, gain_ref, bias_ref, o_ref, oexp_ref, out_ref, u_ref
 ):
     rows_n, cols_n, width = pair_ref.shape
-    w_out = scaled(o_ref, oexp_ref, 1, 0, 1)
+    w_out = twice(scaled(o_ref, oexp_ref, 1, 0, 1))
     gather_lanes(x_ref, u_ref)
     step = 16
     for i in range(0, rows_n, step):
@@ -270,6 +373,7 @@
 
 VMEM = pl.BlockSpec(memory_space=pltpu.VMEM)
 SMEM = pl.BlockSpec(memory_space=pltpu.SMEM)
+ANY = pl.BlockSpec(memory_space=pl.ANY)
 
 
 def call(body, name, specs, outs, scratch, flops, moved):
@@ -293,7 +397,12 @@
     tokens = residue_mask.shape[0]
     bf16, f32 = jnp.bfloat16, jnp.float32
     mask = residue_mask.astype(f32)
-    lane_mask = jnp.tile(mask.reshape(tokens // cols_n, cols_n), (1, own))
+    by_col = mask.reshape(tokens // cols_n, cols_n)
+    lane_mask = jnp.tile(by_col, (1, own))
+    here = lax.axis_index("row") * col_count + lax.axis_index("col")
+    sum_mask = jnp.repeat(jnp.roll(by_col, here, axis=1), own, axis=1)
+    lane = jnp.arange(width, dtype=jnp.int32)[None, :]
+    turn = lane // parts * parts + (lane - here) % parts
     row_mask = jnp.broadcast_to(mask[:, None], (tokens, width))
 
     block = (rows_n, cols_n, width)
@@ -314,17 +423,28 @@
     def product(layer, got):
         return call(
             functools.partial(product_kernel, layer, row_count, own), f"product{layer}",
-            [VMEM, VMEM, VMEM], back, [],
+            [VMEM] * 5, back, [],
             2 * tokens * tokens * tokens * own * own, 6 * pairs * width,
-        )(got, lane_mask, row_mask)
+        )(got, sum_mask, lane_mask, row_mask, turn)
 
     def exchange(x):
         return lax.all_to_all(x, AXES, 0, 0, tiled=True)
 
     turned = pltpu.VMEM((cols_n, rows_n, width), bf16)
     send = call(
-        open_kernel, "open", [VMEM, VMEM, VMEM, VMEM, SMEM], sent,
-        [pltpu.VMEM(block, f32), turned, turned], *proj_cost,
+        open_kernel, "open", [ANY] * 5, sent,
+        [
+            side,
+            pltpu.VMEM(norm_gain.shape, f32),
+            pltpu.VMEM(norm_bias.shape, f32),
+            pltpu.VMEM(w_in_q.shape, bf16),
+            pltpu.SMEM(exp_in.shape, jnp.int32),
+            pltpu.VMEM((rows_n * cols_n, width), f32),
+            turned,
+            turned,
+            pltpu.SemaphoreType.DMA((5,)),
+        ],
+        *proj_cost,
     )(pair, norm_gain, norm_bias, w_in_q, exp_in)
     got = exchange(send)
     gate0 = gate(0, pair)

time: 125 us -> 120 us (0.960)
  Pallas kernels: 21.7 us -> 17.7 us
  waiting for transfers between devices: 54.4 us -> 52.8 us
    pallas_call x1, Pallas kernels: 6.53 us -> 4.27 us  [fast(): call(middle_kernel, 'middle', [VMEM] * 6 + [SMEM, VMEM, SMEM], (jax.Shape...]
    pallas_call x1, Pallas kernels: 5.89 us -> 4.09 us  [fast(): call(open_kernel, 'open', [ANY] * 5, sent, [side, pltpu.VMEM(norm_gain.sh...]
    all_to_all x3, waiting for transfers between devices: 54.4 us -> 52.8 us  [exchange(): return lax.all_to_all(x, AXES, 0, 0, tiled=True)]
  transfers between devices with their start and end apart: 3 -> 3, of which waited for: 3 -> 3; matrix products, arithmetic and copies ran while one was open for 0% -> 0% of each run, Pallas kernels for 2% -> 3%
where the time goes in v2:
time: 120 us
  waiting for transfers between devices  52.8 us (44%)
  blocking collectives  29 us (24%)
  Pallas kernels  17.7 us (15%)
  starting transfers between devices  14.6 us (12%)
  local copies, waits for them, and re-layouts  5.23 us (4%)
    all_to_all x3, waiting for transfers between devices, exchange(): return lax.all_to_all(x, AXES, 0, 0, tiled=True)  52.8 us
    all_to_all x1, blocking collectives, exchange(): return lax.all_to_all(x, AXES, 0, 0, tiled=True)  29 us
    all_to_all x3, starting transfers between devices, exchange(): return lax.all_to_all(x, AXES, 0, 0, tiled=True)  14.6 us
    unnamed x26, local copies, waits for them, and re-layouts  4.77 us
    pallas_call x1, Pallas kernels, fast(): call(middle_kernel, 'middle', [VMEM] * 6 + [SMEM, VMEM, SMEM], (jax.Shape...  4.27 us
    pallas_call x1, Pallas kernels, fast(): call(open_kernel, 'open', [ANY] * 5, sent, [side, pltpu.VMEM(norm_gain.sh...  4.09 us
    pallas_call x2, Pallas kernels, product(): call(functools.partial(product_kernel, layer, row_count, own), f'product{...  3.43 us
    pallas_call x2, Pallas kernels, gate(): call(functools.partial(gate_kernel, layer), f'gate{layer}', [VMEM, VMEM,...  3.32 us
  transfers between devices with their start and end apart: 3, of which 3 were waited for; matrix products, arithmetic and copies ran while one was open for 0% of the time, Pallas kernels for 3%

profile of v2, /device:TPU:0, one launch (start us, length us, event | category | flops | bytes accessed | tf_op | source)
XLA Modules:
  0.0 119.6 jit_solution(12362681994558096887)
XLA Ops:
  0.0 0.0 copy-start
  0.0 1.0 copy-done
  1.0 0.0 copy-start.2
  1.0 1.0 copy-done.2
  2.0 0.0 copy-start.5
  2.0 0.7 copy-done.5
  2.7 0.0 copy-start.7
  2.7 0.7 copy-done.7
  3.4 0.0 copy-start.9
  3.4 0.7 copy-done.9
  4.1 4.1 %open.1 = bf16[32,128,128]{2,1,0:T(8,128)(2,1)} custom-call(bf16[64,32,128]{2,1,0:T(8,128)(2,1)S(1)} %copy-done.2, f32[2,2,128]{2,1,0:T(2,128)S(1)} %copy-done.7, f32[2,2,128]{2,1,0:T(2,128)S(1)} %copy-done.9, bf16[2,128,640]{2,1,0:T(8,128)(2,1)S(1)} %copy-done, s32[2,4,20]{2,1,0:T(4,128)S(1)} %copy-done.5), custom_call_target="tpu_custom_call" | custom-call | flops 268435456 | bytes 2097152 | tf_op jit(solution)/shard_map/open/pallas_call | solution.py:434
  8.2 7.3 %all-to-all-start = ((bf16[32,128,128]{2,1,0:T(8,128)(2,1)}), bf16[32,128,128]{2,1,0:T(8,128)(2,1)S(1)}, u32[]{:S(2)}, u32[]{:S(2)}) async-start(bf16[32,128,128]{2,1,0:T(8,128)(2,1)} %open.1), calls=%async_computation | async-start | bytes 2097152 | tf_op jit(solution)/shard_map/all_to_all | solution.py:431
  15.5 0.0 copy-start.12
  15.5 0.7 copy-done.12
  16.2 0.1 reshape.124
  16.3 0.1 pad_maximum_fusion
  16.4 0.1 constant_dynamic-slice_fusion
  16.4 0.1 copy.12
  16.5 0.1 tile.9.lane_ref
  16.7 25.0 %all-to-all-done.got_ref = bf16[32,128,128]{2,1,0:T(8,128)(2,1)S(1)} async-done(((bf16[32,128,128]{2,1,0:T(8,128)(2,1)}), bf16[32,128,128]{2,1,0:T(8,128)(2,1)S(1)}, u32[]{:S(2)}, u32[]{:S(2)}) %all-to-all-start) | async-done | bytes 1048608 | tf_op jit(solution)/shard_map/all_to_all | solution.py:431
  41.7 0.1 broadcast_in_dim.5.row_ref
  41.8 1.7 %product0.1 = bf16[32,64,128]{2,1,0:T(8,128)(2,1)} custom-call(bf16[32,128,128]{2,1,0:T(8,128)(2,1)S(1)} %all-to-all-done.got_ref, f32[8,128]{1,0:T(8,128)S(1)} %copy.13.sum_ref, f32[8,128]{1,0:T(8,128)S(1)} %tile.9.lane_ref, f32[256,128]{1,0:T(8,128)S(1)} %broadcast_in_dim.5.row_ref, s32[1,128]{1,0:T(1,128)S(1)} %fusion.turn_ref), custom_call_target="tpu_custom_call" | custom-call | flops 536870912 | bytes 1572864 | tf_op jit(solution)/shard_map/product0/pallas_call | solution.py:424
  43.5 0.0 copy-start.1
  43.5 0.0 copy-start.3
  43.5 0.0 copy-start.6
  43.5 0.0 copy-start.8
  43.5 0.0 copy-start.10
  43.5 3.6 %all-to-all-start.1 = ((bf16[32,64,128]{2,1,0:T(8,128)(2,1)}), bf16[32,64,128]{2,1,0:T(8,128)(2,1)S(1)}, u32[]{:S(2)}, u32[]{:S(2)}) async-start(bf16[32,64,128]{2,1,0:T(8,128)(2,1)} %product0.1), calls=%async_computation.1 | async-start | bytes 1048576 | tf_op jit(solution)/shard_map/all_to_all | solution.py:431
  47.2 0.0 copy-done.1
  47.2 0.0 copy-done.3
  47.2 0.0 copy-done.6
  47.2 0.0 copy-done.8
  47.2 0.0 copy-done.10
  47.2 0.0 copy-start.4
  47.2 0.0 copy-start.11
  47.2 1.7 %gate0.1.gate_ref = f32[64,32,128]{2,1,0:T(8,128)S(1)} custom-call(bf16[64,32,128]{2,1,0:T(8,128)(2,1)S(1)} %copy-done.3, f32[2,2,128]{2,1,0:T(2,128)S(1)} %copy-done.8, f32[2,2,128]{2,1,0:T(2,128)S(1)} %copy-done.10, bf16[2,128,640]{2,1,0:T(8,128)(2,1)S(1)} %copy-done.1, s32[2,4,20]{2,1,0:T(4,128)S(1)} %copy-done.6), custom_call_target="tpu_custom_call" | custom-call | flops 67108864 | bytes 2097152 | tf_op jit(solution)/shard_map/gate0/pallas_call | solution.py:417
  48.9 13.9 %all-to-all-done.1.x_ref = bf16[32,64,128]{2,1,0:T(8,128)(2,1)S(1)} async-done(((bf16[32,64,128]{2,1,0:T(8,128)(2,1)}), bf16[32,64,128]{2,1,0:T(8,128)(2,1)S(1)}, u32[]{:S(2)}, u32[]{:S(2)}) %all-to-all-start.1) | async-done | bytes 524320 | tf_op jit(solution)/shard_map/all_to_all | solution.py:431
  62.8 0.0 copy-done.4
  62.8 0.0 copy-done.11
  62.8 4.3 %middle.1 = (bf16[64,32,128]{2,1,0:T(8,128)(2,1)S(1)}, bf16[32,128,128]{2,1,0:T(8,128)(2,1)S(1)}) custom-call(bf16[32,64,128]{2,1,0:T(8,128)(2,1)S(1)} %all-to-all-done.1.x_ref, bf16[64,32,128]{2,1,0:T(8,128)(2,1)S(1)} %copy-done.3, f32[64,32,128]{2,1,0:T(8,128)S(1)} %gate0.1.gate_ref, f32[2,2,128]{2,1,0:T(2,128)S(1)} %copy-done.8, ...), custom_call_target="tpu_custom_call" | custom-call | flops 268435456 | bytes 2097152 | tf_op jit(solution)/shard_map/middle/pallas_call | solution.py:452
  67.1 29.0 %all_to_all.20.got_ref = bf16[32,128,128]{2,1,0:T(8,128)(2,1)S(1)} all-to-all(bf16[32,128,128]{2,1,0:T(8,128)(2,1)S(1)} %get-tuple-element.7), channel_id=1, replica_groups=mesh['row'=4,'col'=8] {'row','col'}, dimensions={0} | all-to-all | bytes 2097152 | tf_op jit(solution)/shard_map/all_to_all | solution.py:431
  96.1 1.7 %product1.1 = bf16[32,64,128]{2,1,0:T(8,128)(2,1)} custom-call(bf16[32,128,128]{2,1,0:T(8,128)(2,1)S(1)} %all_to_all.20.got_ref, f32[8,128]{1,0:T(8,128)S(1)} %copy.13.sum_ref, f32[8,128]{1,0:T(8,128)S(1)} %tile.9.lane_ref, f32[256,128]{1,0:T(8,128)S(1)} %broadcast_in_dim.5.row_ref, s32[1,128]{1,0:T(1,128)S(1)} %fusion.turn_ref), custom_call_target="tpu_custom_call" | custom-call | flops 536870912 | bytes 1572864 | tf_op jit(solution)/shard_map/product1/pallas_call | solution.py:424
  97.8 3.6 %all-to-all-start.3 = ((bf16[32,64,128]{2,1,0:T(8,128)(2,1)}), bf16[32,64,128]{2,1,0:T(8,128)(2,1)S(1)}, u32[]{:S(2)}, u32[]{:S(2)}) async-start(bf16[32,64,128]{2,1,0:T(8,128)(2,1)} %product1.1), calls=%async_computation.3 | async-start | bytes 1048576 | tf_op jit(solution)/shard_map/all_to_all | solution.py:431
  101.4 1.7 %gate1.1.gate_ref = f32[64,32,128]{2,1,0:T(8,128)S(1)} custom-call(bf16[64,32,128]{2,1,0:T(8,128)(2,1)S(1)} %get-tuple-element.8.pair_ref, f32[2,2,128]{2,1,0:T(2,128)S(1)} %copy-done.8, f32[2,2,128]{2,1,0:T(2,128)S(1)} %copy-done.10, bf16[2,128,640]{2,1,0:T(8,128)(2,1)S(1)} %copy-done.1, s32[2,4,20]{2,1,0:T(4,128)S(1)} %copy-done.6), custom_call_target="tpu_custom_call" | custom-call | flops 67108864 | bytes 2097152 | tf_op jit(solution)/shard_map/gate1/pallas_call | solution.py:417
  103.1 13.9 %all-to-all-done.3.x_ref = bf16[32,64,128]{2,1,0:T(8,128)(2,1)S(1)} async-done(((bf16[32,64,128]{2,1,0:T(8,128)(2,1)}), bf16[32,64,128]{2,1,0:T(8,128)(2,1)S(1)}, u32[]{:S(2)}, u32[]{:S(2)}) %all-to-all-start.3) | async-done | bytes 524320 | tf_op jit(solution)/shard_map/all_to_all | solution.py:431
  117.0 2.6 %close.1 = bf16[64,32,128]{2,1,0:T(8,128)(2,1)} custom-call(bf16[32,64,128]{2,1,0:T(8,128)(2,1)S(1)} %all-to-all-done.3.x_ref, bf16[64,32,128]{2,1,0:T(8,128)(2,1)S(1)} %get-tuple-element.8.pair_ref, f32[64,32,128]{2,1,0:T(8,128)S(1)} %gate1.1.gate_ref, f32[2,2,128]{2,1,0:T(2,128)S(1)} %copy-done.8, f32[2,2,128]{2,1,0:T(2,128)S(1)} %copy-done.10, ...), custom_call_target="tpu_custom_call" | custom-call | flops 268435456 | bytes 2097152 | tf_op jit(solution)/shard_map/close/pallas_call | solution.py:459
  (5 shorter events, 0.1 us)
Async XLA Ops:
  0.0 1.0 copy-start
  1.0 1.0 copy-start.2
  2.0 0.7 copy-start.5
  2.7 0.7 copy-start.7
  3.4 0.7 copy-start.9
  8.2 33.5 %all-to-all-start = ((bf16[32,128,128]{2,1,0:T(8,128)(2,1)}), bf16[32,128,128]{2,1,0:T(8,128)(2,1)S(1)}, u32[]{:S(2)}, u32[]{:S(2)}) async-start(bf16[32,128,128]{2,1,0:T(8,128)(2,1)} %open.1), calls=%async_computation | async-start | bytes 2097152 | tf_op jit(solution)/shard_map/all_to_all | solution.py:431
  15.5 0.7 copy-start.12
  43.5 3.6 %copy-start.1 = (bf16[2,128,640]{2,1,0:T(8,128)(2,1)S(1)}, bf16[2,128,640]{2,1,0:T(8,128)(2,1)}, u32[]{:S(2)}) copy-start(bf16[2,128,640]{2,1,0:T(8,128)(2,1)} %q_ref.5) | copy-start | bytes 983044
  43.5 3.7 %copy-start.3 = (bf16[64,32,128]{2,1,0:T(8,128)(2,1)S(1)}, bf16[64,32,128]{2,1,0:T(8,128)(2,1)}, u32[]{:S(2)}) copy-start(bf16[64,32,128]{2,1,0:T(8,128)(2,1)} %pair_ref.3) | copy-start | bytes 1572868
  43.5 3.7 %copy-start.6 = (s32[2,4,20]{2,1,0:T(4,128)S(1)}, s32[2,4,20]{2,1,0:T(4,128)}, u32[]{:S(2)}) copy-start(s32[2,4,20]{2,1,0:T(4,128)} %exp_ref.5) | copy-start | bytes 1924
  43.5 3.7 %copy-start.8 = (f32[2,2,128]{2,1,0:T(2,128)S(1)}, f32[2,2,128]{2,1,0:T(2,128)}, u32[]{:S(2)}) copy-start(f32[2,2,128]{2,1,0:T(2,128)} %gain_ref.7) | copy-start | bytes 6148
  43.5 3.7 %copy-start.10 = (f32[2,2,128]{2,1,0:T(2,128)S(1)}, f32[2,2,128]{2,1,0:T(2,128)}, u32[]{:S(2)}) copy-start(f32[2,2,128]{2,1,0:T(2,128)} %bias_ref.7) | copy-start | bytes 6148
  43.5 19.2 %all-to-all-start.1 = ((bf16[32,64,128]{2,1,0:T(8,128)(2,1)}), bf16[32,64,128]{2,1,0:T(8,128)(2,1)S(1)}, u32[]{:S(2)}, u32[]{:S(2)}) async-start(bf16[32,64,128]{2,1,0:T(8,128)(2,1)} %product0.1), calls=%async_computation.1 | async-start | bytes 1048576 | tf_op jit(solution)/shard_map/all_to_all | solution.py:431
  47.2 15.6 %copy-start.4 = (bf16[2,128,128]{2,1,0:T(8,128)(2,1)S(1)}, bf16[2,128,128]{2,1,0:T(8,128)(2,1)}, u32[]{:S(2)}) copy-start(bf16[2,128,128]{2,1,0:T(8,128)(2,1)} %o_ref.3) | copy-start | bytes 196612
  47.2 15.6 %copy-start.11 = (s32[2,4,4]{2,1,0:T(4,128)S(1)}, s32[2,4,4]{2,1,0:T(4,128)}, u32[]{:S(2)}) copy-start(s32[2,4,4]{2,1,0:T(4,128)} %oexp_ref.3) | copy-start | bytes 388
  97.8 19.2 %all-to-all-start.3 = ((bf16[32,64,128]{2,1,0:T(8,128)(2,1)}), bf16[32,64,128]{2,1,0:T(8,128)(2,1)S(1)}, u32[]{:S(2)}, u32[]{:S(2)}) async-start(bf16[32,64,128]{2,1,0:T(8,128)(2,1)} %product1.1), calls=%async_computation.3 | async-start | bytes 1048576 | tf_op jit(solution)/shard_map/all_to_all | solution.py:431

commit v3 on v2

--- a/solution.py
+++ b/solution.py
@@ -207,6 +207,20 @@
                     send_ref[d, at : at + PACK, :] = got[-d % size]
 
 
+OPEN_STEP = 16
+
+
+CLOSE_STEP = 32
+
+
+def in_turn(count, first, second):
+    ready = first(0)
+    for n in range(count):
+        following = first(n + 1) if n + 1 < count else None
+        second(n, ready)
+        ready = following
+
+
 def open_kernel(
     pair_hbm, gain_hbm, bias_hbm, q_hbm, exp_hbm, send_ref,
     pair_ref, gain_ref, bias_ref, q_ref, exp_ref, t_ref, l_ref, r_ref, sems,
@@ -216,38 +230,54 @@
         for n, (source, target) in enumerate(
             (
                 (exp_hbm, exp_ref),
-                (q_hbm, q_ref),
-                (pair_hbm, pair_ref),
+                (q_hbm.at[0:1, :, 0 : q_ref.shape[2]], q_ref),
                 (gain_hbm, gain_ref),
                 (bias_hbm, bias_ref),
+                (pair_hbm, pair_ref),
             )
         )
     ]
     for move in moves:
         move.start()
-    for move in moves:
+    for move in moves[:-1]:
         move.wait()
     rows_n, cols_n, width = pair_ref.shape
     size = send_ref.shape[0]
     weights = slotted(scaled(q_ref, exp_ref, 0, 0, 4), width, size)
     gain, bias = gain_ref[0, 0:1, :], bias_ref[0, 0:1, :]
+    moves[-1].wait()
     t_ref[...] = pair_ref[...].astype(jnp.float32).reshape(t_ref.shape)
-    step = 8
-    for k in range(0, cols_n, step):
+    step = OPEN_STEP
+
+    def norm(n):
         part = jnp.concatenate(
-            [t_ref[pl.ds(k + s, rows_n, stride=cols_n), :] for s in range(step)], axis=0
-        )
-        part = part.astype(jnp.bfloat16)
-        left, right = gated(norm_rows(part, gain, bias), weights, width)
-        put_rolled(l_ref, k, left, rows_n, size)
-        put_rolled(r_ref, k, right, rows_n, size)
+            [
+                t_ref[pl.ds(n * step + s, rows_n, stride=cols_n), :]
+                for s in range(step)
+            ],
+            axis=0,
+        )
+        return norm_rows(part.astype(jnp.bfloat16), gain, bias)
+
+    def project(n, normed):
+        left, right = gated(normed, weights, width)
+        put_rolled(l_ref, n * step, left, rows_n, size)
+        put_rolled(r_ref, n * step, right, rows_n, size)
+
+    in_turn(cols_n // step, norm, project)
     scatter_lanes(l_ref, r_ref, send_ref)
 
 
-def gate_kernel(layer, pair_ref, gain_ref, bias_ref, q_ref, exp_ref, gate_ref):
+def gate_kernel(
+    layer, size, pair_ref, gain_ref, bias_ref, q_ref, exp_ref, o_ref, oexp_ref,
+    gate_ref, out_ref, *next_ref,
+):
     rows_n, cols_n, width = pair_ref.shape
     weights = twice(scaled(q_ref, exp_ref, layer, 4, 1))
     gain, bias = gain_ref[layer, 0:1, :], bias_ref[layer, 0:1, :]
+    out_ref[...] = twice(scaled(o_ref, oexp_ref, layer, 0, 1))
+    if next_ref:
+        next_ref[0][...] = slotted(scaled(q_ref, exp_ref, layer + 1, 0, 4), width, size)
     step = 16
     for i in range(0, rows_n, step):
         part = beside(pair_ref[i : i + step].reshape(step * cols_n, width))
@@ -340,43 +370,42 @@
 
 
 def middle_kernel(
-    x_ref, pair_ref, gate_ref, gain_ref, bias_ref, q_ref, exp_ref, o_ref, oexp_ref,
+    x_ref, pair_ref, gate_ref, w_out_ref, w_in_ref, gain_ref, bias_ref,
     mid_ref, send_ref, u_ref, l_ref, r_ref,
 ):
     rows_n, cols_n, width = pair_ref.shape
-    w_out = twice(scaled(o_ref, oexp_ref, 0, 0, 1))
     size = send_ref.shape[0]
-    weights = slotted(scaled(q_ref, exp_ref, 1, 0, 4), width, size)
-    gain, bias = gain_ref[1, 0:1, :], bias_ref[1, 0:1, :]
     gather_lanes(x_ref, u_ref)
-    step = 16
-    for i in range(0, rows_n, step):
-        mid = finish_rows(0, i, step, u_ref, pair_ref, gate_ref, gain_ref, bias_ref, w_out)
-        mid_ref[i : i + step] = mid.reshape(step, cols_n, width)
-        left, right = gated(norm_rows(mid, gain, bias), weights, width)
-        put_rolled(l_ref, i, left, cols_n, size)
-        put_rolled(r_ref, i, right, cols_n, size)
+    mid = finish_rows(
+        0, 0, rows_n, u_ref, pair_ref, gate_ref, gain_ref, bias_ref, w_out_ref[...]
+    )
+    mid_ref[...] = mid.reshape(rows_n, cols_n, width)
+    normed = norm_rows(mid, gain_ref[1, 0:1, :], bias_ref[1, 0:1, :])
+    left, right = gated(normed, w_in_ref[...], width)
+    put_rolled(l_ref, 0, left, cols_n, size)
+    put_rolled(r_ref, 0, right, cols_n, size)
     scatter_lanes(l_ref, r_ref, send_ref)
 
 
 def close_kernel(
-    x_ref, pair_ref, gate_ref, gain_ref, bias_ref, o_ref, oexp_ref, out_ref, u_ref
+    x_ref, pair_ref, gate_ref, w_out_ref, gain_ref, bias_ref, out_ref, u_ref
 ):
     rows_n, cols_n, width = pair_ref.shape
-    w_out = twice(scaled(o_ref, oexp_ref, 1, 0, 1))
     gather_lanes(x_ref, u_ref)
-    step = 16
+    step = CLOSE_STEP
     for i in range(0, rows_n, step):
-        out = finish_rows(1, i, step, u_ref, pair_ref, gate_ref, gain_ref, bias_ref, w_out)
+        out = finish_rows(
+            1, i, step, u_ref, pair_ref, gate_ref, gain_ref, bias_ref, w_out_ref[...]
+        )
         out_ref[i : i + step] = out.reshape(step, cols_n, width)
 
 
 VMEM = pl.BlockSpec(memory_space=pltpu.VMEM)
 SMEM = pl.BlockSpec(memory_space=pltpu.SMEM)
-ANY = pl.BlockSpec(memory_space=pl.ANY)
-
-
-def call(body, name, specs, outs, scratch, flops, moved):
+HBM = pl.BlockSpec(memory_space=pltpu.HBM)
+
+
+def call(body, name, specs, outs, scratch, flops, moved, grant=40 * 2**20):
     return pl.pallas_call(
         body,
         name=name,
@@ -385,7 +414,7 @@
         out_shape=outs,
         scratch_shapes=scratch,
         cost_estimate=pl.CostEstimate(flops=flops, bytes_accessed=moved, transcendentals=0),
-        compiler_params=pltpu.CompilerParams(vmem_limit_bytes=40 * 2**20),
+        compiler_params=pltpu.CompilerParams(vmem_limit_bytes=grant),
     )
 
 
@@ -411,14 +440,18 @@
     pairs = rows_n * cols_n
     proj_cost = (2 * pairs * width * 4 * width, 8 * pairs * width)
     side = pltpu.VMEM(block, bf16)
-    gate_out = jax.ShapeDtypeStruct(block, f32)
+    gate_outs = (
+        jax.ShapeDtypeStruct(block, f32),
+        jax.ShapeDtypeStruct((2 * width, 2 * width), bf16),
+        jax.ShapeDtypeStruct((width, 4 * width), bf16),
+    )
 
     def gate(layer, source):
         return call(
-            functools.partial(gate_kernel, layer), f"gate{layer}",
-            [VMEM, VMEM, VMEM, VMEM, SMEM], gate_out, [],
+            functools.partial(gate_kernel, layer, parts), f"gate{layer}",
+            [VMEM, VMEM, VMEM, VMEM, SMEM, VMEM, SMEM], gate_outs[: 3 - layer], [],
             2 * pairs * width * width, 8 * pairs * width,
-        )(source, norm_gain, norm_bias, w_in_q, exp_in)
+        )(source, norm_gain, norm_bias, w_in_q, exp_in, w_out_q, exp_out)
 
     def product(layer, got):
         return call(
@@ -432,34 +465,34 @@
 
     turned = pltpu.VMEM((cols_n, rows_n, width), bf16)
     send = call(
-        open_kernel, "open", [ANY] * 5, sent,
+        open_kernel, "open", [HBM] * 5, sent,
         [
             side,
             pltpu.VMEM(norm_gain.shape, f32),
             pltpu.VMEM(norm_bias.shape, f32),
-            pltpu.VMEM(w_in_q.shape, bf16),
+            pltpu.VMEM((1, width, 4 * width), bf16),
             pltpu.SMEM(exp_in.shape, jnp.int32),
             pltpu.VMEM((rows_n * cols_n, width), f32),
             turned,
             turned,
             pltpu.SemaphoreType.DMA((5,)),
         ],
-        *proj_cost,
+        *proj_cost, grant=None,
     )(pair, norm_gain, norm_bias, w_in_q, exp_in)
     got = exchange(send)
-    gate0 = gate(0, pair)
+    gate0, w_out, w_in = gate(0, pair)
     x = exchange(product(0, got))
     mid, send = call(
-        middle_kernel, "middle", [VMEM] * 6 + [SMEM, VMEM, SMEM],
+        middle_kernel, "middle", [VMEM] * 7,
         (jax.ShapeDtypeStruct(block, bf16), sent), [side, side, side], *proj_cost,
-    )(x, pair, gate0, norm_gain, norm_bias, w_in_q, exp_in, w_out_q, exp_out)
+    )(x, pair, gate0, w_out, w_in, norm_gain, norm_bias)
     got = exchange(send)
-    gate1 = gate(1, mid)
+    gate1, w_out = gate(1, mid)
     x = exchange(product(1, got))
     return call(
-        close_kernel, "close", [VMEM] * 6 + [SMEM],
+        close_kernel, "close", [VMEM] * 6,
         jax.ShapeDtypeStruct(block, bf16), [side], *proj_cost,
-    )(x, mid, gate1, norm_gain, norm_bias, w_out_q, exp_out)
+    )(x, mid, gate1, w_out, norm_gain, norm_bias)
 
 
 def solution(mesh):

time: 120 us -> 113 us (0.942)
  local copies, waits for them, and re-layouts: 5.23 us -> 1.17 us
  Pallas kernels: 17.7 us -> 14.6 us
    unnamed x26 -> x16, local copies, waits for them, and re-layouts: 4.77 us -> 0.7 us
    pallas_call x5, Pallas kernels: 14.2 us -> 11.2 us  [the longest x1 3.86 us: fast(): call(open_kernel, 'open', [HBM] * 5, sent, [side, pltpu.VMEM(norm_gain.sh...]
where the time goes in v3:
time: 113 us; the launch traced here: 112 us
  waiting for transfers between devices  52.6 us (47%)
  blocking collectives  29 us (26%)
  Pallas kernels  14.6 us (13%)
  starting transfers between devices  14.6 us (13%)
  local copies, waits for them, and re-layouts  1.17 us (1%)
    all_to_all x3, waiting for transfers between devices, exchange(): return lax.all_to_all(x, AXES, 0, 0, tiled=True)  52.6 us
    all_to_all x1, blocking collectives, exchange(): return lax.all_to_all(x, AXES, 0, 0, tiled=True)  29 us
    all_to_all x3, starting transfers between devices, exchange(): return lax.all_to_all(x, AXES, 0, 0, tiled=True)  14.6 us
    pallas_call x1, Pallas kernels, fast(): call(open_kernel, 'open', [HBM] * 5, sent, [side, pltpu.VMEM(norm_gain.sh...  3.86 us
    pallas_call x2, Pallas kernels, gate(): call(functools.partial(gate_kernel, layer, parts), f'gate{layer}', [VMEM,...  3.51 us
    pallas_call x2, Pallas kernels, product(): call(functools.partial(product_kernel, layer, row_count, own), f'product{...  3.42 us
  transfers between devices with their start and end apart: 3, of which 3 were waited for; matrix products, arithmetic and copies ran while one was open for 0% of the time, Pallas kernels for 3%

profile of v3, /device:TPU:0, one launch (start us, length us, event | category | flops | bytes accessed | tf_op | source)
XLA Modules:
  0.0 112.3 jit_solution(16430727544028397371)
XLA Ops:
  0.0 3.9 %open.1 = bf16[32,128,128]{2,1,0:T(8,128)(2,1)} custom-call(bf16[64,32,128]{2,1,0:T(8,128)(2,1)} %pair_ref.3, f32[2,2,128]{2,1,0:T(2,128)} %gain_ref.7, f32[2,2,128]{2,1,0:T(2,128)} %bias_ref.7, bf16[2,128,640]{2,1,0:T(8,128)(2,1)} %q_ref.3, s32[2,4,20]{2,1,0:T(4,128)} %exp_ref.3), custom_call_target="tpu_custom_call" | custom-call | flops 268435456 | bytes 2097152 | tf_op jit(solution)/shard_map/open/pallas_call | solution.py:467
  3.9 7.3 %all-to-all-start = ((bf16[32,128,128]{2,1,0:T(8,128)(2,1)}), bf16[32,128,128]{2,1,0:T(8,128)(2,1)S(1)}, u32[]{:S(2)}, u32[]{:S(2)}) async-start(bf16[32,128,128]{2,1,0:T(8,128)(2,1)} %open.1), calls=%async_computation | async-start | bytes 2097152 | tf_op jit(solution)/shard_map/all_to_all | solution.py:464
  11.2 0.0 copy-start.7
  11.2 0.7 copy-done.7
  11.9 0.1 reshape.124
  12.0 0.1 pad_maximum_fusion
  12.1 0.1 constant_dynamic-slice_fusion
  12.1 0.1 copy.12
  12.2 0.1 tile.9.lane_ref
  12.4 25.0 %all-to-all-done.got_ref = bf16[32,128,128]{2,1,0:T(8,128)(2,1)S(1)} async-done(((bf16[32,128,128]{2,1,0:T(8,128)(2,1)}), bf16[32,128,128]{2,1,0:T(8,128)(2,1)S(1)}, u32[]{:S(2)}, u32[]{:S(2)}) %all-to-all-start) | async-done | bytes 1048608 | tf_op jit(solution)/shard_map/all_to_all | solution.py:464
  37.4 0.1 broadcast_in_dim.5.row_ref
  37.5 1.7 %product0.1 = bf16[32,64,128]{2,1,0:T(8,128)(2,1)} custom-call(bf16[32,128,128]{2,1,0:T(8,128)(2,1)S(1)} %all-to-all-done.got_ref, f32[8,128]{1,0:T(8,128)S(1)} %copy.13.sum_ref, f32[8,128]{1,0:T(8,128)S(1)} %tile.9.lane_ref, f32[256,128]{1,0:T(8,128)S(1)} %broadcast_in_dim.5.row_ref, s32[1,128]{1,0:T(1,128)S(1)} %fusion.turn_ref), custom_call_target="tpu_custom_call" | custom-call | flops 536870912 | bytes 1572864 | tf_op jit(solution)/shard_map/product0/pallas_call | solution.py:457
  39.2 0.0 copy-start
  39.2 0.0 copy-start.1
  39.2 0.0 copy-start.2
  39.2 0.0 copy-start.3
  39.2 0.0 copy-start.4
  39.2 0.0 copy-start.5
  39.3 0.0 copy-start.6
  39.3 3.6 %all-to-all-start.1 = ((bf16[32,64,128]{2,1,0:T(8,128)(2,1)}), bf16[32,64,128]{2,1,0:T(8,128)(2,1)S(1)}, u32[]{:S(2)}, u32[]{:S(2)}) async-start(bf16[32,64,128]{2,1,0:T(8,128)(2,1)} %product0.1), calls=%async_computation.1 | async-start | bytes 1048576 | tf_op jit(solution)/shard_map/all_to_all | solution.py:464
  42.9 0.0 copy-done
  42.9 0.0 copy-done.1
  42.9 0.0 copy-done.2
  42.9 0.0 copy-done.3
  42.9 0.0 copy-done.4
  43.0 0.0 copy-done.5
  43.0 0.0 copy-done.6
  43.0 1.8 %gate0.1 = (f32[64,32,128]{2,1,0:T(8,128)S(1)}, bf16[256,256]{1,0:T(8,128)(2,1)S(1)}, bf16[128,512]{1,0:T(8,128)(2,1)S(1)}) custom-call(bf16[64,32,128]{2,1,0:T(8,128)(2,1)S(1)} %copy-done, f32[2,2,128]{2,1,0:T(2,128)S(1)} %copy-done.3, f32[2,2,128]{2,1,0:T(2,128)S(1)} %copy-done.4, bf16[2,128,640]{2,1,0:T(8,128)(2,1)S(1)} %copy-done.1, ...), custom_call_target="tpu_custom_call" | custom-call | flops 67108864 | bytes 2097152 | tf_op jit(solution)/shard_map/gate0/pallas_call | solution.py:450
  44.8 13.7 %all-to-all-done.1.x_ref = bf16[32,64,128]{2,1,0:T(8,128)(2,1)S(1)} async-done(((bf16[32,64,128]{2,1,0:T(8,128)(2,1)}), bf16[32,64,128]{2,1,0:T(8,128)(2,1)S(1)}, u32[]{:S(2)}, u32[]{:S(2)}) %all-to-all-start.1) | async-done | bytes 524320 | tf_op jit(solution)/shard_map/all_to_all | solution.py:464
  58.5 2.1 %middle.1 = (bf16[64,32,128]{2,1,0:T(8,128)(2,1)S(1)}, bf16[32,128,128]{2,1,0:T(8,128)(2,1)S(1)}) custom-call(bf16[32,64,128]{2,1,0:T(8,128)(2,1)S(1)} %all-to-all-done.1.x_ref, bf16[64,32,128]{2,1,0:T(8,128)(2,1)S(1)} %copy-done, f32[64,32,128]{2,1,0:T(8,128)S(1)} %get-tuple-element.12.gate_ref, bf16[256,256]{1,0:T(8,128)(2,1)S(1)} %get-tuple-element.13.w_out_ref, ...), custom_call_target="tpu_custom_call" | custom-call | flops 268435456 | bytes 2097152 | tf_op jit(solution)/shard_map/middle/pallas_call | solution.py:485
  60.6 29.0 %all_to_all.20.got_ref = bf16[32,128,128]{2,1,0:T(8,128)(2,1)S(1)} all-to-all(bf16[32,128,128]{2,1,0:T(8,128)(2,1)S(1)} %get-tuple-element.15), channel_id=1, replica_groups=mesh['row'=4,'col'=8] {'row','col'}, dimensions={0} | all-to-all | bytes 2097152 | tf_op jit(solution)/shard_map/all_to_all | solution.py:464
  89.6 1.7 %product1.1 = bf16[32,64,128]{2,1,0:T(8,128)(2,1)} custom-call(bf16[32,128,128]{2,1,0:T(8,128)(2,1)S(1)} %all_to_all.20.got_ref, f32[8,128]{1,0:T(8,128)S(1)} %copy.13.sum_ref, f32[8,128]{1,0:T(8,128)S(1)} %tile.9.lane_ref, f32[256,128]{1,0:T(8,128)S(1)} %broadcast_in_dim.5.row_ref, s32[1,128]{1,0:T(1,128)S(1)} %fusion.turn_ref), custom_call_target="tpu_custom_call" | custom-call | flops 536870912 | bytes 1572864 | tf_op jit(solution)/shard_map/product1/pallas_call | solution.py:457
  91.3 3.6 %all-to-all-start.3 = ((bf16[32,64,128]{2,1,0:T(8,128)(2,1)}), bf16[32,64,128]{2,1,0:T(8,128)(2,1)S(1)}, u32[]{:S(2)}, u32[]{:S(2)}) async-start(bf16[32,64,128]{2,1,0:T(8,128)(2,1)} %product1.1), calls=%async_computation.3 | async-start | bytes 1048576 | tf_op jit(solution)/shard_map/all_to_all | solution.py:464
  95.0 1.7 %gate1.1 = (f32[64,32,128]{2,1,0:T(8,128)S(1)}, bf16[256,256]{1,0:T(8,128)(2,1)S(1)}) custom-call(bf16[64,32,128]{2,1,0:T(8,128)(2,1)S(1)} %get-tuple-element.16.pair_ref, f32[2,2,128]{2,1,0:T(2,128)S(1)} %copy-done.3, f32[2,2,128]{2,1,0:T(2,128)S(1)} %copy-done.4, bf16[2,128,640]{2,1,0:T(8,128)(2,1)S(1)} %copy-done.1, s32[2,4,20]{2,1,0:T(4,128)S(1)} %copy-done.5, ...), custom_call_target="tpu_custom_call" | custom-call | flops 67108864 | bytes 2097152 | tf_op jit(solution)/shard_map/gate1/pallas_call | solution.py:450
  96.7 13.9 %all-to-all-done.3.x_ref = bf16[32,64,128]{2,1,0:T(8,128)(2,1)S(1)} async-done(((bf16[32,64,128]{2,1,0:T(8,128)(2,1)}), bf16[32,64,128]{2,1,0:T(8,128)(2,1)S(1)}, u32[]{:S(2)}, u32[]{:S(2)}) %all-to-all-start.3) | async-done | bytes 524320 | tf_op jit(solution)/shard_map/all_to_all | solution.py:464
  110.6 1.7 %close.1 = bf16[64,32,128]{2,1,0:T(8,128)(2,1)} custom-call(bf16[32,64,128]{2,1,0:T(8,128)(2,1)S(1)} %all-to-all-done.3.x_ref, bf16[64,32,128]{2,1,0:T(8,128)(2,1)S(1)} %get-tuple-element.16.pair_ref, f32[64,32,128]{2,1,0:T(8,128)S(1)} %get-tuple-element.17.gate_ref, bf16[256,256]{1,0:T(8,128)(2,1)S(1)} %get-tuple-element.18.w_out_ref, ...), custom_call_target="tpu_custom_call" | custom-call | flops 268435456 | bytes 2097152 | tf_op jit(solution)/shard_map/close/pallas_call | solution.py:492
  (5 shorter events, 0.1 us)
Async XLA Ops:
  3.9 33.5 %all-to-all-start = ((bf16[32,128,128]{2,1,0:T(8,128)(2,1)}), bf16[32,128,128]{2,1,0:T(8,128)(2,1)S(1)}, u32[]{:S(2)}, u32[]{:S(2)}) async-start(bf16[32,128,128]{2,1,0:T(8,128)(2,1)} %open.1), calls=%async_computation | async-start | bytes 2097152 | tf_op jit(solution)/shard_map/all_to_all | solution.py:464
  11.2 0.7 copy-start.7
  39.2 3.7 %copy-start = (bf16[64,32,128]{2,1,0:T(8,128)(2,1)S(1)}, bf16[64,32,128]{2,1,0:T(8,128)(2,1)}, u32[]{:S(2)}) copy-start(bf16[64,32,128]{2,1,0:T(8,128)(2,1)} %pair_ref.3) | copy-start | bytes 1572868
  39.2 3.7 %copy-start.1 = (bf16[2,128,640]{2,1,0:T(8,128)(2,1)S(1)}, bf16[2,128,640]{2,1,0:T(8,128)(2,1)}, u32[]{:S(2)}) copy-start(bf16[2,128,640]{2,1,0:T(8,128)(2,1)} %q_ref.3) | copy-start | bytes 983044
  39.2 3.7 %copy-start.2 = (bf16[2,128,128]{2,1,0:T(8,128)(2,1)S(1)}, bf16[2,128,128]{2,1,0:T(8,128)(2,1)}, u32[]{:S(2)}) copy-start(bf16[2,128,128]{2,1,0:T(8,128)(2,1)} %o_ref.3) | copy-start | bytes 196612
  39.2 3.7 %copy-start.3 = (f32[2,2,128]{2,1,0:T(2,128)S(1)}, f32[2,2,128]{2,1,0:T(2,128)}, u32[]{:S(2)}) copy-start(f32[2,2,128]{2,1,0:T(2,128)} %gain_ref.7) | copy-start | bytes 6148
  39.2 3.7 %copy-start.4 = (f32[2,2,128]{2,1,0:T(2,128)S(1)}, f32[2,2,128]{2,1,0:T(2,128)}, u32[]{:S(2)}) copy-start(f32[2,2,128]{2,1,0:T(2,128)} %bias_ref.7) | copy-start | bytes 6148
  39.2 3.7 %copy-start.5 = (s32[2,4,20]{2,1,0:T(4,128)S(1)}, s32[2,4,20]{2,1,0:T(4,128)}, u32[]{:S(2)}) copy-start(s32[2,4,20]{2,1,0:T(4,128)} %exp_ref.3) | copy-start | bytes 1924
  39.3 3.7 %copy-start.6 = (s32[2,4,4]{2,1,0:T(4,128)S(1)}, s32[2,4,4]{2,1,0:T(4,128)}, u32[]{:S(2)}) copy-start(s32[2,4,4]{2,1,0:T(4,128)} %oexp_ref.3) | copy-start | bytes 388
  39.3 19.2 %all-to-all-start.1 = ((bf16[32,64,128]{2,1,0:T(8,128)(2,1)}), bf16[32,64,128]{2,1,0:T(8,128)(2,1)S(1)}, u32[]{:S(2)}, u32[]{:S(2)}) async-start(bf16[32,64,128]{2,1,0:T(8,128)(2,1)} %product0.1), calls=%async_computation.1 | async-start | bytes 1048576 | tf_op jit(solution)/shard_map/all_to_all | solution.py:464
  91.3 19.2 %all-to-all-start.3 = ((bf16[32,64,128]{2,1,0:T(8,128)(2,1)}), bf16[32,64,128]{2,1,0:T(8,128)(2,1)S(1)}, u32[]{:S(2)}, u32[]{:S(2)}) async-start(bf16[32,64,128]{2,1,0:T(8,128)(2,1)} %product1.1), calls=%async_computation.3 | async-start | bytes 1048576 | tf_op jit(solution)/shard_map/all_to_all | solution.py:464
